TPU v7x, 32 devices: a whole 2x2x4 slice. The times are simulated.
32 devices in a mesh: gx: 4 (over z), gy: 8 (over y, x, core).
Axes of the slice: x: 2, y: 2, z: 4, core: 2. Of those that a mesh axis runs over, the one named last changes fastest.
Arguments:
- sensitivity: float32 [3, 262144], P(None, ('gx', 'gy')), may hold values from -24 to 24
- node_weight: float32 [262144], P(('gx', 'gy')), may hold values from 0.05 to 0.5
- dest_device: int32 [262144, 1], P(('gx', 'gy')), may hold values from 0 to 31; in each aligned block of 8192 rows (0 to 8191, 8192 to 16383, ...) at most 512 rows name the same one
- dest_cell: int32 [262144], P(('gx', 'gy')), may hold values from 0 to 131071
- box_owner: int32 [262144, 1], P(('gx', 'gy')), may hold values from 0 to 31; in each aligned block of 8192 rows (0 to 8191, 8192 to 16383, ...) at most 512 rows name the same one
- box_slot: int32 [262144], P(('gx', 'gy')), may hold values from 0 to 63
- stiffness: float32 [64, 256, 256], P('gx', 'gy'), may hold values from 0.5 to 2
- anchor: float32 [3, 64, 256, 256], P(None, 'gx', 'gy'), may hold values from 3 to 6
- coupling: float32 [9, 64, 256, 256], P(None, 'gx', 'gy'), may hold values from -1 to 1
Outputs:
- adjoint: float32 [3, 64, 256, 256], P(None, 'gx', 'gy')
- box_gradient: float32 [3, 2048], P(None, ('gx', 'gy'))
Inputs may be any that keep to these rules, and one draw needn't show every extreme that they name: `dest_device`: among the rows of one device, no deformation device is named more than 512 times, and in some device's rows one is named exactly 512 times. `box_owner`: among the rows of one device, no owner is named more than 512 times, and in some device's rows one is named exactly 512 times.
All inputs are finite; a program needn't handle non-finite values.
Results may differ from a plain program's by a relative error of at most 0.0003.
Values sent between devices are 32-bit elements; how exact they have to be, the bound alone decides.
A program may use at most 192 MiB of HBM per device.

v0:
```python
import functools

import jax
import jax.numpy as jnp
from jax import lax
from jax.experimental import pallas as pl
from jax.experimental.pallas import tpu as pltpu
from jax.sharding import PartitionSpec as P

BOX_DEV = 64
SWEEPS = 4
SENT = 6
NT = (((1,), (1,)), ((), ()))
F32 = jnp.float32
BF16 = jnp.bfloat16
MESH = pl.DeviceIdType.MESH


def two_terms(x):
    hi = x.astype(BF16).astype(F32)
    return hi, x - hi


def matches(count, row):
    return lax.broadcasted_iota(jnp.int32, (count, row.shape[1]), 0) == row


def one_hot(mask):
    return jnp.where(mask, 1.0, 0.0).astype(BF16)


def scaled(mask, row):
    return jnp.where(mask, row, 0.0).astype(BF16)


def dot_nt(a, b):
    return lax.dot_general(a, b, NT, preferred_element_type=F32)


def pack_kernel(step, sens, weight, device, cell, owner, slot, out, tri, seen):
    targets, fields, capacity = out.shape
    rows = sens.shape[1]
    out[...] = jnp.zeros_like(out)
    seen[...] = jnp.zeros_like(seen)
    tri[...] = one_hot(
        lax.broadcasted_iota(jnp.int32, (step, step), 0)
        < lax.broadcasted_iota(jnp.int32, (step, step), 1)
    )

    def block(index, carry):
        span = pl.ds(pl.multiple_of(index * step, step), step)
        target = device[:, span]
        chosen = matches(targets, target)
        before = jnp.dot(one_hot(chosen), tri[...], preferred_element_type=F32) + seen[:, :1]
        rank = jnp.sum(jnp.where(chosen, before, 0.0), axis=0, keepdims=True).astype(jnp.int32)
        seen[...] = seen[...] + jnp.sum(jnp.where(chosen, 1.0, 0.0), axis=1, keepdims=True)
        place = one_hot(matches(capacity, rank))
        payload = jnp.concatenate(
            [
                sens[:, span],
                cell[:, span].astype(F32),
                weight[:, span],
                (owner[:, span] * BOX_DEV + slot[:, span]).astype(F32),
                jnp.zeros((fields - SENT, step), F32),
            ],
            axis=0,
        )
        wide = (targets, fields, step)
        to = lax.broadcasted_iota(jnp.int32, wide, 0) == target[None]
        terms = [
            jnp.where(to, term[None], 0.0).reshape(targets * fields, step).astype(BF16)
            for term in two_terms(payload)
        ]
        product = dot_nt(jnp.concatenate(terms, axis=0), place)
        product = product[: targets * fields] + product[targets * fields :]
        out[...] = out[...] + product.reshape(targets, fields, capacity)
        return carry

    lax.fori_loop(0, rows // step, block, 0)


def pack_rows(devices, capacity, sens, weight, device, cell, owner, slot):
    step = min(2048, sens.shape[1])
    return pl.pallas_call(
        functools.partial(pack_kernel, step),
        out_shape=jax.ShapeDtypeStruct((devices, 8, capacity), F32),
        in_specs=[pl.BlockSpec(memory_space=pltpu.VMEM)] * 6,
        out_specs=pl.BlockSpec(memory_space=pltpu.VMEM),
        scratch_shapes=[pltpu.VMEM((step, step), BF16), pltpu.VMEM((devices, 128), F32)],
        name="pack_rows",
    )(sens, weight, device, cell, owner, slot)


def joined(ref):
    return jnp.concatenate([ref[i, :SENT] for i in range(ref.shape[0])], axis=1)


def scatter_kernel(arrived, load, total):
    parts, size_xy, size_z = load.shape

    @pl.when(pl.program_id(0) == 0)
    def _():
        total[...] = jnp.zeros_like(total)

    block = joined(arrived)
    cell = block[3:4].astype(jnp.int32)
    at_z = matches(size_z, cell % size_z)
    at_xy = one_hot(matches(size_xy, cell // size_z))
    pairs = [two_terms(block[k : k + 1]) for k in range(parts)]
    terms = [scaled(at_z, hi) for hi, lo in pairs] + [scaled(at_z, lo) for hi, lo in pairs]
    product = dot_nt(jnp.concatenate(terms, axis=0), at_xy)
    half = parts * size_z
    total[...] = total[...] + product[:half] + product[half:]

    @pl.when(pl.program_id(0) == pl.num_programs(0) - 1)
    def _():
        for k in range(parts):
            load[k] = total[k * size_z : (k + 1) * size_z].T


def scatter_rows(arrived, group, size_xy, size_z):
    devices, fields, capacity = arrived.shape
    return pl.pallas_call(
        scatter_kernel,
        grid=(devices // group,),
        out_shape=jax.ShapeDtypeStruct((3, size_xy, size_z), F32),
        in_specs=[pl.BlockSpec((group, fields, capacity), lambda i: (i, 0, 0))],
        out_specs=pl.BlockSpec((3, size_xy, size_z), lambda i: (0, 0, 0)),
        scratch_shapes=[pltpu.VMEM((3 * size_z, size_xy), F32)],
        name="scatter_rows",
    )(arrived)


def gather_kernel(arrived, field, boxes, terms):
    parts, size_xy, size_z = field.shape
    devices = boxes.shape[0]

    @pl.when(pl.program_id(0) == 0)
    def _():
        boxes[...] = jnp.zeros_like(boxes)
        for k in range(parts):
            hi, lo = two_terms(field[k].T)
            terms[k * size_z : (k + 1) * size_z] = hi.astype(BF16)
            terms[(parts + k) * size_z : (parts + k + 1) * size_z] = lo.astype(BF16)

    block = joined(arrived)
    cell = block[3:4].astype(jnp.int32)
    at_z = matches(size_z, cell % size_z)
    at_xy = one_hot(matches(size_xy, cell // size_z))
    columns = jnp.dot(terms[...], at_xy, preferred_element_type=F32)
    box = block[5:6].astype(jnp.int32)
    at_owner = one_hot(matches(devices, box // BOX_DEV))
    at_slot = matches(BOX_DEV, box % BOX_DEV)
    for k in range(parts):
        column = columns[k * size_z : (k + 1) * size_z]
        column = column + columns[(parts + k) * size_z : (parts + k + 1) * size_z]
        value = jnp.sum(jnp.where(at_z, column, 0.0), axis=0, keepdims=True) * block[4:5]
        hi, lo = two_terms(value)
        part = dot_nt(at_owner, scaled(at_slot, hi)) + dot_nt(at_owner, scaled(at_slot, lo))
        boxes[:, k * BOX_DEV : (k + 1) * BOX_DEV] += part


def gather_rows(arrived, group, field):
    devices, fields, capacity = arrived.shape
    parts, size_xy, size_z = field.shape
    return pl.pallas_call(
        gather_kernel,
        grid=(devices // group,),
        out_shape=jax.ShapeDtypeStruct((devices, 3 * BOX_DEV), F32),
        in_specs=[
            pl.BlockSpec((group, fields, capacity), lambda i: (i, 0, 0)),
            pl.BlockSpec(memory_space=pltpu.VMEM),
        ],
        out_specs=pl.BlockSpec((devices, 3 * BOX_DEV), lambda i: (0, 0)),
        scratch_shapes=[pltpu.VMEM((2 * parts * size_z, size_xy), BF16)],
        name="gather_rows",
    )(arrived, field)


def sweep_kernel(load, stiff, anchor, coupling, adjoint, weighted, rest, inverse, edge, halo, x_send, x_recv, y_send, y_recv):
    parts, size_x, size_y, size_z = load.shape
    exchanges = weighted.shape[0]
    gx, gy = lax.axis_index("gx"), lax.axis_index("gy")
    last_x, last_y = lax.axis_size("gx") - 1, lax.axis_size("gy") - 1
    sides = (("gx", gx, -1, gx > 0), ("gx", gx, 1, gx < last_x), ("gy", gy, -1, gy > 0), ("gy", gy, 1, gy < last_y))
    y_at = lax.broadcasted_iota(jnp.int32, (size_y, size_z), 0)
    z_at = lax.broadcasted_iota(jnp.int32, (size_y, size_z), 1)

    for index in range(exchanges):
        for k in range(parts):
            weighted[index, k, 0] = jnp.zeros((size_y, size_z), F32)
            weighted[index, k, size_x + 1] = jnp.zeros((size_y, size_z), F32)
    halo[...] = jnp.zeros_like(halo)

    barrier = pltpu.get_barrier_semaphore()
    known = 0
    for axis, place, move, present in sides:
        known = known + present.astype(jnp.int32)

        @pl.when(present)
        def _():
            pl.semaphore_signal(barrier, inc=1, device_id={axis: place + move}, device_id_type=MESH)

    pl.semaphore_wait(barrier, known)

    def copies(index):
        made = []
        for side, (axis, place, move, present) in enumerate(sides):
            there = 1 - side % 2
            if axis == "gx":
                pair = (weighted.at[index, :, 1 if move < 0 else size_x], weighted.at[index, :, size_x + 1 if move < 0 else 0])
                sems = (x_send, x_recv)
            else:
                pair = (edge.at[index, side % 2], halo.at[index, there])
                sems = (y_send, y_recv)
            made.append((present, pltpu.make_async_remote_copy(
                src_ref=pair[0],
                dst_ref=pair[1],
                send_sem=sems[0].at[index, side % 2],
                recv_sem=sems[1].at[index, there],
                device_id={axis: place + move},
                device_id_type=MESH,
            )))
        return made

    def arrivals(index):
        made = []
        for side, (axis, place, move, present) in enumerate(sides):
            if axis == "gx":
                pair = (weighted.at[index, :, 1 if move < 0 else size_x], weighted.at[index, :, 0 if move < 0 else size_x + 1])
                sems = (x_send, x_recv)
            else:
                pair = (edge.at[index, side % 2], halo.at[index, side % 2])
                sems = (y_send, y_recv)
            made.append((present, pltpu.make_async_remote_copy(
                src_ref=pair[0],
                dst_ref=pair[1],
                send_sem=sems[0].at[index, side % 2],
                recv_sem=sems[1].at[index, side % 2],
                device_id={axis: place + move},
                device_id_type=MESH,
            )))
        return made

    def publish(index, x, k, value):
        adjoint[k, x] = value
        if index < exchanges:
            product = stiff[x] * value
            weighted[index, k, x + 1] = product
            edge[index, 0, k, pl.ds(x, 1), :] = product[0:1]
            edge[index, 1, k, pl.ds(x, 1), :] = product[size_y - 1 : size_y]

    def first(x, carry):
        for k in range(parts):
            inverse[k, x] = 1.0 / (6.0 * stiff[x] + anchor[k, x] + coupling[4 * k, x])
            publish(0, x, k, load[k, x] * inverse[k, x])
        return carry

    lax.fori_loop(0, size_x, first, 0)
    for index in range(exchanges):
        for present, copy in copies(index):

            @pl.when(present)
            def _():
                copy.start()

        def near(x, carry):
            fields = [adjoint[k, x] for k in range(parts)]
            for k in range(parts):
                product = weighted[index, k, x + 1]
                value = load[k, x] - 6.0 * product - anchor[k, x] * fields[k]
                for j in range(parts):
                    value = value - coupling[3 * j + k, x] * fields[j]
                value = value + jnp.where(z_at == 0, 0.0, pltpu.roll(product, 1, 1))
                value = value + jnp.where(z_at == size_z - 1, 0.0, pltpu.roll(product, size_z - 1, 1))
                value = value + jnp.where(y_at == 0, 0.0, pltpu.roll(product, 1, 0))
                value = value + jnp.where(y_at == size_y - 1, 0.0, pltpu.roll(product, size_y - 1, 0))
                rest[k, x] = value
            return carry

        lax.fori_loop(0, size_x, near, 0)
        for present, copy in arrivals(index):

            @pl.when(present)
            def _():
                copy.wait_recv()

        def far(x, carry):
            for k in range(parts):
                value = rest[k, x] + weighted[index, k, x] + weighted[index, k, x + 2]
                value = value + jnp.where(y_at == 0, halo[index, 0, k, pl.ds(x, 1), :], 0.0)
                value = value + jnp.where(y_at == size_y - 1, halo[index, 1, k, pl.ds(x, 1), :], 0.0)
                publish(index + 1, x, k, adjoint[k, x] + value * inverse[k, x])
            return carry

        lax.fori_loop(0, size_x, far, 0)
    for index in range(exchanges):
        for present, copy in copies(index):

            @pl.when(present)
            def _():
                copy.wait_send()


def solve_sweeps(load, stiffness, anchor, coupling):
    parts, size_x, size_y, size_z = load.shape
    exchanges = SWEEPS - 1
    return pl.pallas_call(
        sweep_kernel,
        out_shape=jax.ShapeDtypeStruct(load.shape, F32),
        in_specs=[pl.BlockSpec(memory_space=pltpu.VMEM)] * 4,
        out_specs=pl.BlockSpec(memory_space=pltpu.VMEM),
        scratch_shapes=[
            pltpu.VMEM((exchanges, parts, size_x + 2, size_y, size_z), F32),
            pltpu.VMEM(load.shape, F32),
            pltpu.VMEM(load.shape, F32),
            pltpu.VMEM((exchanges, 2, parts, size_x, size_z), F32),
            pltpu.VMEM((exchanges, 2, parts, size_x, size_z), F32),
        ]
        + [pltpu.SemaphoreType.DMA((exchanges, 2))] * 4,
        compiler_params=pltpu.CompilerParams(collective_id=0, has_side_effects=True),
        name="sweeps",
    )(load, stiffness, anchor, coupling)


def exchange_kernel(live, send, recv, send_sem, recv_sem, own_sem):
    count = send.shape[0]
    width = lax.axis_size("gy")
    me = lax.axis_index("gx") * width + lax.axis_index("gy")
    barrier = pltpu.get_barrier_semaphore()

    def device(index):
        return (index // width, index % width)

    def greet(step, carry):
        pl.semaphore_signal(barrier, inc=1, device_id=device((me + step) % count), device_id_type=MESH)
        return carry

    lax.fori_loop(1, count, greet, 0)
    pl.semaphore_wait(barrier, count - 1)

    def copy(step, source, landing):
        peer = (me + step) % count
        return pltpu.make_async_remote_copy(
            src_ref=send.at[source, pl.ds(0, live)],
            dst_ref=recv.at[landing, pl.ds(0, live)],
            send_sem=send_sem.at[step],
            recv_sem=recv_sem.at[step],
            device_id=device(peer),
            device_id_type=MESH,
        )

    def start(step, carry):
        copy(step, (me + step) % count, me).start()
        return carry

    lax.fori_loop(1, count, start, 0)
    own = pltpu.make_async_copy(send.at[me, pl.ds(0, live)], recv.at[me, pl.ds(0, live)], own_sem)
    own.start()

    def finish(step, carry):
        copy(step, (me + step) % count, (me + count - step) % count).wait_recv()
        copy(step, (me + step) % count, me).wait_send()
        return carry

    lax.fori_loop(1, count, finish, 0)
    own.wait()


def exchange(blocks, live, number):
    count = blocks.shape[0]
    return pl.pallas_call(
        functools.partial(exchange_kernel, live),
        out_shape=jax.ShapeDtypeStruct(blocks.shape, F32),
        in_specs=[pl.BlockSpec(memory_space=pltpu.VMEM)],
        out_specs=pl.BlockSpec(memory_space=pltpu.VMEM),
        scratch_shapes=[pltpu.SemaphoreType.DMA((count,))] * 2 + [pltpu.SemaphoreType.DMA],
        compiler_params=pltpu.CompilerParams(collective_id=number, has_side_effects=True),
        name="exchange_" + str(number),
    )(blocks)


def body(
    sensitivity,
    node_weight,
    dest_device,
    dest_cell,
    box_owner,
    box_slot,
    stiffness,
    anchor,
    coupling,
):
    devices = lax.axis_size("gx") * lax.axis_size("gy")
    row_count = sensitivity.shape[1]
    capacity = 2 * row_count // devices
    size_x, size_y, size_z = stiffness.shape
    size_xy = size_x * size_y
    assert size_xy * size_z <= 2**17 and devices * BOX_DEV <= 2**17
    group = max(1, min(devices, 2048 // capacity))

    def row(values):
        return values.reshape(1, row_count)

    packed = pack_rows(
        devices,
        capacity,
        sensitivity,
        row(node_weight),
        row(dest_device),
        row(dest_cell),
        row(box_owner),
        row(box_slot),
    )
    arrived = exchange(packed, SENT, 1)
    load = scatter_rows(arrived, group, size_xy, size_z)
    load = load.reshape(3, size_x, size_y, size_z)
    adjoint = solve_sweeps(load, stiffness, anchor, coupling)
    partial = gather_rows(arrived, group, adjoint.reshape(3, size_xy, size_z))
    partial = exchange(partial.reshape(devices, 1, 3 * BOX_DEV), 1, 2)
    box_gradient = jnp.sum(partial, axis=(0, 1)).reshape(3, BOX_DEV)
    return (adjoint, box_gradient)


def solution(mesh):
    placed = (
        P(None, ("gx", "gy")),
        P(("gx", "gy")),
        P(("gx", "gy"), None),
        P(("gx", "gy")),
        P(("gx", "gy"), None),
        P(("gx", "gy")),
        P("gx", "gy", None),
        P(None, "gx", "gy", None),
        P(None, "gx", "gy", None),
    )
    return jax.shard_map(
        body,
        mesh=mesh,
        in_specs=placed,
        out_specs=(P(None, "gx", "gy", None), P(None, ("gx", "gy"))),
        check_vma=False,
    )
```

profile of v0, /device:TPU:0, one launch (start us, length us, event | category | flops | bytes accessed | tf_op | source)
XLA Modules:
  0.0 133.7 jit_solution(15552015866364923186)
XLA Ops:
  0.6 13.3 %pack_rows.1.send = f32[32,8,512]{2,1,0:T(8,128)} custom-call(f32[3,8192]{1,0:T(4,128)} %sens.1, f32[1,8192]{1,0:T(1,128)} %bitcast.9, s32[1,8192]{1,0:T(1,128)} %bitcast.10, s32[1,8192]{1,0:T(1,128)} %bitcast.11, s32[1,8192]{1,0:T(1,128)} %bitcast.12, s32[1,8192]{1,0:T(1,128)} %bitcast.13), custom_call_target="tpu_custom_call" | custom-call | tf_op jit(solution)/shard_map/pack_rows/pallas_call | solution.py:84
  14.0 16.3 %exchange_1.1.arrived = f32[32,8,512]{2,1,0:T(8,128)} custom-call(f32[32,8,512]{2,1,0:T(8,128)} %pack_rows.1.send), custom_call_target="tpu_custom_call" | custom-call | tf_op jit(solution)/shard_map/exchange_1/pallas_call | solution.py:372
  30.3 30.3 %scatter_rows.1 = f32[3,512,256]{2,1,0:T(8,128)} custom-call(f32[32,8,512]{2,1,0:T(8,128)} %exchange_1.1.arrived), custom_call_target="tpu_custom_call" | custom-call | tf_op jit(solution)/shard_map/scatter_rows/pallas_call | solution.py:123
  60.6 22.4 %sweeps.1 = f32[3,16,32,256]{3,2,1,0:T(8,128)} custom-call(f32[3,16,32,256]{3,2,1,0:T(8,128)} %bitcast.8, f32[16,32,256]{2,1,0:T(8,128)} %stiff.1, f32[3,16,32,256]{3,2,1,0:T(8,128)} %anchor.1, f32[9,16,32,256]{3,2,1,0:T(8,128)} %coupling.1), custom_call_target="tpu_custom_call" | custom-call | tf_op jit(solution)/shard_map/sweeps/pallas_call | solution.py:308
  83.0 0.0 copy-start
  83.0 36.3 %gather_rows.1 = f32[32,192]{1,0:T(8,128)} custom-call(f32[32,8,512]{2,1,0:T(8,128)} %exchange_1.1.arrived, f32[3,512,256]{2,1,0:T(8,128)} %bitcast.7), custom_call_target="tpu_custom_call" | custom-call | tf_op jit(solution)/shard_map/gather_rows/pallas_call | solution.py:166
  119.4 1.4 %reshape.38.send = f32[32,1,192]{2,1,0:T(1,128)} reshape(f32[32,192]{1,0:T(8,128)} %gather_rows.1) | data formatting | bytes 49152 | tf_op jit(solution)/shard_map/reshape | solution.py:420
  120.7 10.3 %exchange_2.1 = f32[32,1,192]{2,1,0:T(1,128)} custom-call(f32[32,1,192]{2,1,0:T(1,128)} %reshape.38.send), custom_call_target="tpu_custom_call" | custom-call | tf_op jit(solution)/shard_map/exchange_2/pallas_call | solution.py:372
  131.1 0.8 reduce_sum.9
  131.9 0.7 reshape.39
  132.5 0.0 copy-done
  132.5 1.1 copy.12
Async XLA Ops:
  83.0 49.5 %copy-start = (f32[3,16,32,256]{3,2,1,0:T(8,128)S(1)}, f32[3,16,32,256]{3,2,1,0:T(8,128)}, u32[]{:S(2)}) copy-start(f32[3,16,32,256]{3,2,1,0:T(8,128)} %sweeps.1) | copy-start | bytes 4718596
where the time goes:
time: 134 us
  Pallas kernels  129 us (96%)
  local copies, waits for them, and re-layouts  3.19 us (2%)
    pallas_call x1, Pallas kernels, gather_rows(): pl.pallas_call(gather_kernel, grid=(devices // group,), out_shape=jax.Sha...  36.3 us
    pallas_call x1, Pallas kernels, scatter_rows(): pl.pallas_call(scatter_kernel, grid=(devices // group,), out_shape=jax.Sh...  30.3 us
    pallas_call x2, Pallas kernels, exchange(): pl.pallas_call(functools.partial(exchange_kernel, live), out_shape=jax.Sh...  26.6 us
    pallas_call x1, Pallas kernels, solve_sweeps(): pl.pallas_call(sweep_kernel, out_shape=jax.ShapeDtypeStruct(load.shape, F...  22.4 us
    pallas_call x1, Pallas kernels, pack_rows(): pl.pallas_call(functools.partial(pack_kernel, step), out_shape=jax.ShapeD...  13.3 us

commit v1 on v0

--- a/solution.py
+++ b/solution.py
@@ -91,90 +91,186 @@
     )(sens, weight, device, cell, owner, slot)
 
 
-def joined(ref):
-    return jnp.concatenate([ref[i, :SENT] for i in range(ref.shape[0])], axis=1)
-
-
-def scatter_kernel(arrived, load, total):
+def split(value, size):
+    if size & (size - 1) == 0:
+        return value >> (size.bit_length() - 1), value & (size - 1)
+    return value // size, value % size
+
+
+def sort_kernel(cut, slabs, arrived, tiles, ends):
+    senders, fields, capacity = arrived.shape
+    per_group, _, width = tiles.shape
+    join = max(1, min(senders, 512 // capacity))
+    count, length = senders // join, join * capacity
+    blocks = [
+        jnp.concatenate([arrived[q * join + i] for i in range(join)], axis=1)
+        for q in range(count)
+    ]
+    chosen = [matches(slabs, split(block[3:4].astype(jnp.int32), cut)[0]) for block in blocks]
+    stacked = one_hot(jnp.concatenate(chosen, axis=0))
+    total = count * slabs
+    earlier = one_hot(
+        lax.broadcasted_iota(jnp.int32, (length, length), 0)
+        < lax.broadcasted_iota(jnp.int32, (length, length), 1)
+    )
+    before = jnp.dot(stacked, earlier, preferred_element_type=F32)
+    number = jnp.dot(stacked, jnp.ones((length, 128), BF16), preferred_element_type=F32)
+    this = lax.broadcasted_iota(jnp.int32, (total, total), 0)
+    other = lax.broadcasted_iota(jnp.int32, (total, total), 1)
+    ahead = one_hot((other % slabs < this % slabs) | ((other % slabs == this % slabs) & (other < this)))
+    tens = jnp.floor(number * 0.0625)
+    first = 16.0 * jnp.dot(ahead, tens.astype(BF16), preferred_element_type=F32)
+    first = first + jnp.dot(ahead, (number - 16.0 * tens).astype(BF16), preferred_element_type=F32)
+
+    start = first[:slabs]
+    later = lax.broadcasted_iota(jnp.int32, start.shape, 0) > 0
+    begin = (lax.broadcasted_iota(jnp.int32, start.shape, 1) * width).astype(F32)
+    low = jnp.sum(jnp.where(later & (start <= begin), 1.0, 0.0), axis=0, keepdims=True)
+    high = jnp.sum(jnp.where(later & (start < begin + width), 1.0, 0.0), axis=0, keepdims=True)
+    ends[0] = jnp.concatenate([low, high, jnp.zeros((6, 128), F32)], axis=0).astype(jnp.int32)
+
+    sums = jnp.zeros((per_group * 2 * fields, width), F32)
+    for q in range(count):
+        rows = slice(q * slabs, (q + 1) * slabs)
+        where = before[rows] + first[rows, :1]
+        place = jnp.sum(jnp.where(chosen[q], where, 0.0), axis=0, keepdims=True).astype(jnp.int32)
+        tile, lane = split(place, width)
+        terms = jnp.concatenate(two_terms(blocks[q]), axis=0)
+        spread = jnp.concatenate([scaled(tile == t, terms) for t in range(per_group)], axis=0)
+        sums = sums + dot_nt(spread, one_hot(matches(width, lane)))
+    for t in range(per_group):
+        at = t * 2 * fields
+        tiles[t] = sums[at : at + fields] + sums[at + fields : at + 2 * fields]
+
+
+def sort_rows(arrived, slabs, cut):
+    devices, fields, capacity = arrived.shape
+    rows = devices * capacity
+    size = min(4096, rows)
+    width = min(256, size)
+    groups = rows // size
+    return pl.pallas_call(
+        functools.partial(sort_kernel, cut, slabs),
+        grid=(groups,),
+        out_shape=[
+            jax.ShapeDtypeStruct((rows // width, fields, width), F32),
+            jax.ShapeDtypeStruct((groups, 8, 128), jnp.int32),
+        ],
+        in_specs=[pl.BlockSpec((size // capacity, fields, capacity), lambda i: (i, 0, 0))],
+        out_specs=[
+            pl.BlockSpec((size // width, fields, width), lambda i: (i, 0, 0)),
+            pl.BlockSpec((1, 8, 128), lambda i: (i, 0, 0)),
+        ],
+        name="sort_rows",
+    )(arrived)
+
+
+def located(tile, size_z):
+    return split(tile[3:4].astype(jnp.int32), size_z)
+
+
+def scatter_kernel(size_y, ends, tiles, load):
     parts, size_xy, size_z = load.shape
-
-    @pl.when(pl.program_id(0) == 0)
-    def _():
-        total[...] = jnp.zeros_like(total)
-
-    block = joined(arrived)
-    cell = block[3:4].astype(jnp.int32)
-    at_z = matches(size_z, cell % size_z)
-    at_xy = one_hot(matches(size_xy, cell // size_z))
-    pairs = [two_terms(block[k : k + 1]) for k in range(parts)]
-    terms = [scaled(at_z, hi) for hi, lo in pairs] + [scaled(at_z, lo) for hi, lo in pairs]
-    product = dot_nt(jnp.concatenate(terms, axis=0), at_xy)
-    half = parts * size_z
-    total[...] = total[...] + product[:half] + product[half:]
-
-    @pl.when(pl.program_id(0) == pl.num_programs(0) - 1)
-    def _():
+    per_group = tiles.shape[0] // ends.shape[0]
+    half = parts * size_y
+    load[...] = jnp.zeros_like(load)
+
+    def one_tile(t, carry):
+        group, index = t // per_group, t % per_group
+        tile = tiles[t]
+        xy, z = located(tile, size_z)
+        at_z = one_hot(matches(size_z, z))
+        pairs = [two_terms(tile[k : k + 1]) for k in range(parts)]
+        values = [hi for hi, lo in pairs] + [lo for hi, lo in pairs]
+
+        def one_slab(x, carry):
+            at_y = matches(size_y, xy - x * size_y)
+            terms = jnp.concatenate([scaled(at_y, value) for value in values], axis=0)
+            product = dot_nt(terms, at_z)
+            product = product[:half] + product[half:]
+            span = pl.ds(pl.multiple_of(x * size_y, size_y), size_y)
+            for k in range(parts):
+                load[k, span] = load[k, span] + product[k * size_y : (k + 1) * size_y]
+            return carry
+
+        return lax.fori_loop(ends[group, 0, index], ends[group, 1, index] + 1, one_slab, carry)
+
+    lax.fori_loop(0, tiles.shape[0], one_tile, 0)
+
+
+def scatter_rows(tiles, ends, size_x, size_y, size_z):
+    return pl.pallas_call(
+        functools.partial(scatter_kernel, size_y),
+        out_shape=jax.ShapeDtypeStruct((3, size_x * size_y, size_z), F32),
+        in_specs=[pl.BlockSpec(memory_space=pltpu.SMEM), pl.BlockSpec(memory_space=pltpu.VMEM)],
+        out_specs=pl.BlockSpec(memory_space=pltpu.VMEM),
+        name="scatter_rows",
+    )(ends, tiles)
+
+
+def gather_kernel(ends, tiles, field, boxes, terms, sums):
+    parts, size_x, size_y, size_z = field.shape
+    per_group = tiles.shape[0] // ends.shape[0]
+    devices = boxes.shape[0]
+    half = parts * size_y
+    width = tiles.shape[2]
+    sums[...] = jnp.zeros_like(sums)
+
+    def cut(x, carry):
         for k in range(parts):
-            load[k] = total[k * size_z : (k + 1) * size_z].T
-
-
-def scatter_rows(arrived, group, size_xy, size_z):
-    devices, fields, capacity = arrived.shape
-    return pl.pallas_call(
-        scatter_kernel,
-        grid=(devices // group,),
-        out_shape=jax.ShapeDtypeStruct((3, size_xy, size_z), F32),
-        in_specs=[pl.BlockSpec((group, fields, capacity), lambda i: (i, 0, 0))],
-        out_specs=pl.BlockSpec((3, size_xy, size_z), lambda i: (0, 0, 0)),
-        scratch_shapes=[pltpu.VMEM((3 * size_z, size_xy), F32)],
-        name="scatter_rows",
-    )(arrived)
-
-
-def gather_kernel(arrived, field, boxes, terms):
-    parts, size_xy, size_z = field.shape
-    devices = boxes.shape[0]
-
-    @pl.when(pl.program_id(0) == 0)
-    def _():
-        boxes[...] = jnp.zeros_like(boxes)
-        for k in range(parts):
-            hi, lo = two_terms(field[k].T)
-            terms[k * size_z : (k + 1) * size_z] = hi.astype(BF16)
-            terms[(parts + k) * size_z : (parts + k + 1) * size_z] = lo.astype(BF16)
-
-    block = joined(arrived)
-    cell = block[3:4].astype(jnp.int32)
-    at_z = matches(size_z, cell % size_z)
-    at_xy = one_hot(matches(size_xy, cell // size_z))
-    columns = jnp.dot(terms[...], at_xy, preferred_element_type=F32)
-    box = block[5:6].astype(jnp.int32)
-    at_owner = one_hot(matches(devices, box // BOX_DEV))
-    at_slot = matches(BOX_DEV, box % BOX_DEV)
+            hi, lo = two_terms(field[k, x])
+            terms[x, k * size_y : (k + 1) * size_y] = hi.astype(BF16)
+            terms[x, half + k * size_y : half + (k + 1) * size_y] = lo.astype(BF16)
+        return carry
+
+    lax.fori_loop(0, size_x, cut, 0)
+
+    def one_tile(t, carry):
+        group, index = t // per_group, t % per_group
+        tile = tiles[t]
+        xy, z = located(tile, size_z)
+        at_z = one_hot(matches(size_z, z))
+
+        def one_slab(x, found):
+            at_y = matches(size_y, xy - x * size_y)
+            columns = jnp.dot(terms[x], at_z, preferred_element_type=F32)
+            columns = columns[:half] + columns[half:]
+            return tuple(
+                found[k] + jnp.sum(jnp.where(at_y, columns[k * size_y : (k + 1) * size_y], 0.0).reshape(size_y // 8, 8, width), axis=0)
+                for k in range(parts)
+            )
+
+        empty = tuple(jnp.zeros((8, width), F32) for _ in range(parts))
+        found = lax.fori_loop(ends[group, 0, index], ends[group, 1, index] + 1, one_slab, empty)
+        owner, slot = split(tile[5:6].astype(jnp.int32), BOX_DEV)
+        at_owner = matches(devices, owner)
+        pairs = [two_terms(jnp.sum(part, axis=0, keepdims=True) * tile[4:5]) for part in found]
+        values = [hi for hi, lo in pairs] + [lo for hi, lo in pairs]
+        spread = jnp.concatenate([scaled(at_owner, value) for value in values], axis=0)
+        sums[...] = sums[...] + dot_nt(spread, one_hot(matches(BOX_DEV, slot)))
+        return carry
+
+    lax.fori_loop(0, tiles.shape[0], one_tile, 0)
     for k in range(parts):
-        column = columns[k * size_z : (k + 1) * size_z]
-        column = column + columns[(parts + k) * size_z : (parts + k + 1) * size_z]
-        value = jnp.sum(jnp.where(at_z, column, 0.0), axis=0, keepdims=True) * block[4:5]
-        hi, lo = two_terms(value)
-        part = dot_nt(at_owner, scaled(at_slot, hi)) + dot_nt(at_owner, scaled(at_slot, lo))
-        boxes[:, k * BOX_DEV : (k + 1) * BOX_DEV] += part
-
-
-def gather_rows(arrived, group, field):
-    devices, fields, capacity = arrived.shape
-    parts, size_xy, size_z = field.shape
+        part = sums[k * devices : (k + 1) * devices] + sums[(parts + k) * devices : (parts + k + 1) * devices]
+        boxes[:, k * BOX_DEV : (k + 1) * BOX_DEV] = part
+
+
+def gather_rows(tiles, ends, field):
+    groups = ends.shape[0]
+    parts, size_x, size_y, size_z = field.shape
+    devices = lax.axis_size("gx") * lax.axis_size("gy")
     return pl.pallas_call(
         gather_kernel,
-        grid=(devices // group,),
         out_shape=jax.ShapeDtypeStruct((devices, 3 * BOX_DEV), F32),
-        in_specs=[
-            pl.BlockSpec((group, fields, capacity), lambda i: (i, 0, 0)),
-            pl.BlockSpec(memory_space=pltpu.VMEM),
+        in_specs=[pl.BlockSpec(memory_space=pltpu.SMEM)] + [pl.BlockSpec(memory_space=pltpu.VMEM)] * 2,
+        out_specs=pl.BlockSpec(memory_space=pltpu.VMEM),
+        scratch_shapes=[
+            pltpu.VMEM((size_x, 2 * parts * size_y, size_z), BF16),
+            pltpu.VMEM((2 * parts * devices, BOX_DEV), F32),
         ],
-        out_specs=pl.BlockSpec((devices, 3 * BOX_DEV), lambda i: (0, 0)),
-        scratch_shapes=[pltpu.VMEM((2 * parts * size_z, size_xy), BF16)],
         name="gather_rows",
-    )(arrived, field)
+    )(ends, tiles, field)
 
 
 def sweep_kernel(load, stiff, anchor, coupling, adjoint, weighted, rest, inverse, edge, halo, x_send, x_recv, y_send, y_recv):
@@ -268,9 +364,10 @@
             fields = [adjoint[k, x] for k in range(parts)]
             for k in range(parts):
                 product = weighted[index, k, x + 1]
-                value = load[k, x] - 6.0 * product - anchor[k, x] * fields[k]
+                value = load[k, x]
                 for j in range(parts):
-                    value = value - coupling[3 * j + k, x] * fields[j]
+                    if j != k:
+                        value = value - coupling[3 * j + k, x] * fields[j]
                 value = value + jnp.where(z_at == 0, 0.0, pltpu.roll(product, 1, 1))
                 value = value + jnp.where(z_at == size_z - 1, 0.0, pltpu.roll(product, size_z - 1, 1))
                 value = value + jnp.where(y_at == 0, 0.0, pltpu.roll(product, 1, 0))
@@ -290,7 +387,7 @@
                 value = rest[k, x] + weighted[index, k, x] + weighted[index, k, x + 2]
                 value = value + jnp.where(y_at == 0, halo[index, 0, k, pl.ds(x, 1), :], 0.0)
                 value = value + jnp.where(y_at == size_y - 1, halo[index, 1, k, pl.ds(x, 1), :], 0.0)
-                publish(index + 1, x, k, adjoint[k, x] + value * inverse[k, x])
+                publish(index + 1, x, k, value * inverse[k, x])
             return carry
 
         lax.fori_loop(0, size_x, far, 0)
@@ -397,7 +494,6 @@
     size_x, size_y, size_z = stiffness.shape
     size_xy = size_x * size_y
     assert size_xy * size_z <= 2**17 and devices * BOX_DEV <= 2**17
-    group = max(1, min(devices, 2048 // capacity))
 
     def row(values):
         return values.reshape(1, row_count)
@@ -413,10 +509,11 @@
         row(box_slot),
     )
     arrived = exchange(packed, SENT, 1)
-    load = scatter_rows(arrived, group, size_xy, size_z)
+    tiles, ends = sort_rows(arrived, size_x, size_y * size_z)
+    load = scatter_rows(tiles, ends, size_x, size_y, size_z)
     load = load.reshape(3, size_x, size_y, size_z)
     adjoint = solve_sweeps(load, stiffness, anchor, coupling)
-    partial = gather_rows(arrived, group, adjoint.reshape(3, size_xy, size_z))
+    partial = gather_rows(tiles, ends, adjoint)
     partial = exchange(partial.reshape(devices, 1, 3 * BOX_DEV), 1, 2)
     box_gradient = jnp.sum(partial, axis=(0, 1)).reshape(3, BOX_DEV)
     return (adjoint, box_gradient)

time: 134 us -> 144 us (1.075)
  Pallas kernels: 129 us -> 139 us
    pallas_call x2 -> x3, Pallas kernels: 66.6 us -> 76.3 us  [the longest x1 38.6 us: gather_rows(): pl.pallas_call(gather_kernel, out_shape=jax.ShapeDtypeStruct((devices, 3...]
where the time goes in v1:
time: 144 us
  Pallas kernels  139 us (97%)
  local copies, waits for them, and re-layouts  3.19 us (2%)
    pallas_call x1, Pallas kernels, gather_rows(): pl.pallas_call(gather_kernel, out_shape=jax.ShapeDtypeStruct((devices, 3...  38.6 us
    pallas_call x1, Pallas kernels, scatter_rows(): pl.pallas_call(functools.partial(scatter_kernel, size_y), out_shape=jax.S...  31 us
    pallas_call x2, Pallas kernels, exchange(): pl.pallas_call(functools.partial(exchange_kernel, live), out_shape=jax.Sh...  26.9 us
    pallas_call x1, Pallas kernels, solve_sweeps(): pl.pallas_call(sweep_kernel, out_shape=jax.ShapeDtypeStruct(load.shape, F...  22.4 us
    pallas_call x1, Pallas kernels, pack_rows(): pl.pallas_call(functools.partial(pack_kernel, step), out_shape=jax.ShapeD...  13.3 us
    pallas_call x1, Pallas kernels, sort_rows(): pl.pallas_call(functools.partial(sort_kernel, cut, slabs), grid=(groups,)...  6.7 us

profile of v1, /device:TPU:0, one launch (start us, length us, event | category | flops | bytes accessed | tf_op | source)
XLA Modules:
  0.0 143.6 jit_solution(15856199178457981448)
XLA Ops:
  0.6 13.3 %pack_rows.1.send = f32[32,8,512]{2,1,0:T(8,128)} custom-call(f32[3,8192]{1,0:T(4,128)} %sens.1, f32[1,8192]{1,0:T(1,128)} %bitcast.7, s32[1,8192]{1,0:T(1,128)} %bitcast.8, s32[1,8192]{1,0:T(1,128)} %bitcast.9, s32[1,8192]{1,0:T(1,128)} %bitcast.10, s32[1,8192]{1,0:T(1,128)} %bitcast.11), custom_call_target="tpu_custom_call" | custom-call | tf_op jit(solution)/shard_map/pack_rows/pallas_call | solution.py:84
  14.0 16.3 %exchange_1.1.arrived = f32[32,8,512]{2,1,0:T(8,128)} custom-call(f32[32,8,512]{2,1,0:T(8,128)} %pack_rows.1.send), custom_call_target="tpu_custom_call" | custom-call | tf_op jit(solution)/shard_map/exchange_1/pallas_call | solution.py:469
  30.2 6.7 %sort_rows.1 = (f32[64,8,256]{2,1,0:T(8,128)}, s32[4,8,128]{2,1,0:T(8,128)}) custom-call(f32[32,8,512]{2,1,0:T(8,128)} %exchange_1.1.arrived), custom_call_target="tpu_custom_call" | custom-call | tf_op jit(solution)/shard_map/sort_rows/pallas_call | solution.py:152
  36.9 31.0 %scatter_rows.1 = f32[3,512,256]{2,1,0:T(8,128)} custom-call(s32[4,8,128]{2,1,0:T(8,128)} %get-tuple-element.4.ends, f32[64,8,256]{2,1,0:T(8,128)} %get-tuple-element.5.tiles), custom_call_target="tpu_custom_call" | custom-call | tf_op jit(solution)/shard_map/scatter_rows/pallas_call | solution.py:202
  68.0 22.4 %sweeps.1.field = f32[3,16,32,256]{3,2,1,0:T(8,128)} custom-call(f32[3,16,32,256]{3,2,1,0:T(8,128)} %bitcast.6, f32[16,32,256]{2,1,0:T(8,128)} %stiff.1, f32[3,16,32,256]{3,2,1,0:T(8,128)} %anchor.1, f32[9,16,32,256]{3,2,1,0:T(8,128)} %coupling.1), custom_call_target="tpu_custom_call" | custom-call | tf_op jit(solution)/shard_map/sweeps/pallas_call | solution.py:405
  90.4 0.0 copy-start
  90.4 38.6 %gather_rows.1 = f32[32,192]{1,0:T(8,128)} custom-call(s32[4,8,128]{2,1,0:T(8,128)} %get-tuple-element.4.ends, f32[64,8,256]{2,1,0:T(8,128)} %get-tuple-element.5.tiles, f32[3,16,32,256]{3,2,1,0:T(8,128)} %sweeps.1.field), custom_call_target="tpu_custom_call" | custom-call | tf_op jit(solution)/shard_map/gather_rows/pallas_call | solution.py:263
  129.0 1.4 reshape.34.send
  130.3 10.6 %exchange_2.1 = f32[32,1,192]{2,1,0:T(1,128)} custom-call(f32[32,1,192]{2,1,0:T(1,128)} %reshape.34.send), custom_call_target="tpu_custom_call" | custom-call | tf_op jit(solution)/shard_map/exchange_2/pallas_call | solution.py:469
  141.0 0.8 reduce_sum.9
  141.8 0.7 reshape.35
  142.5 0.0 copy-done
  142.5 1.1 copy.12
Async XLA Ops:
  90.4 52.1 %copy-start = (f32[3,16,32,256]{3,2,1,0:T(8,128)S(1)}, f32[3,16,32,256]{3,2,1,0:T(8,128)}, u32[]{:S(2)}) copy-start(f32[3,16,32,256]{3,2,1,0:T(8,128)} %sweeps.1.field) | copy-start | bytes 4718596

commit v2 on v1

--- a/solution.py
+++ b/solution.py
@@ -97,6 +97,18 @@
     return value // size, value % size
 
 
+def wide_matches(count, row):
+    return lax.broadcasted_iota(jnp.int16, (count, row.shape[1]), 0) == row.astype(jnp.int16)
+
+
+def wide_one_hot(count, row):
+    return jnp.where(wide_matches(count, row), jnp.array(1, BF16), jnp.array(0, BF16))
+
+
+def kept(mask, values):
+    return jnp.where(mask, values, jnp.array(0, BF16))
+
+
 def sort_kernel(cut, slabs, arrived, tiles, ends):
     senders, fields, capacity = arrived.shape
     per_group, _, width = tiles.shape
@@ -122,12 +134,14 @@
     first = 16.0 * jnp.dot(ahead, tens.astype(BF16), preferred_element_type=F32)
     first = first + jnp.dot(ahead, (number - 16.0 * tens).astype(BF16), preferred_element_type=F32)
 
+    steps = per_group + slabs - 1
     start = first[:slabs]
-    later = lax.broadcasted_iota(jnp.int32, start.shape, 0) > 0
-    begin = (lax.broadcasted_iota(jnp.int32, start.shape, 1) * width).astype(F32)
-    low = jnp.sum(jnp.where(later & (start <= begin), 1.0, 0.0), axis=0, keepdims=True)
-    high = jnp.sum(jnp.where(later & (start < begin + width), 1.0, 0.0), axis=0, keepdims=True)
-    ends[0] = jnp.concatenate([low, high, jnp.zeros((6, 128), F32)], axis=0).astype(jnp.int32)
+    row = lax.broadcasted_iota(jnp.int32, start.shape, 0).astype(F32)
+    step = lax.broadcasted_iota(jnp.int32, start.shape, 1).astype(F32)
+    entry = row + jnp.minimum(jnp.floor(start * (1.0 / width)), per_group - 1.0)
+    slab = jnp.sum(jnp.where((row > 0) & (entry <= step), 1.0, 0.0), axis=0, keepdims=True)
+    slab = jnp.where(step[:1] < steps, slab, slabs)
+    ends[0] = jnp.broadcast_to(slab, (8, 128)).astype(jnp.int32)
 
     sums = jnp.zeros((per_group * 2 * fields, width), F32)
     for q in range(count):
@@ -135,9 +149,10 @@
         where = before[rows] + first[rows, :1]
         place = jnp.sum(jnp.where(chosen[q], where, 0.0), axis=0, keepdims=True).astype(jnp.int32)
         tile, lane = split(place, width)
-        terms = jnp.concatenate(two_terms(blocks[q]), axis=0)
-        spread = jnp.concatenate([scaled(tile == t, terms) for t in range(per_group)], axis=0)
-        sums = sums + dot_nt(spread, one_hot(matches(width, lane)))
+        terms = jnp.concatenate(two_terms(blocks[q]), axis=0).astype(BF16)
+        tile = jnp.broadcast_to(tile, terms.shape).astype(jnp.int16)
+        spread = jnp.concatenate([kept(tile == t, terms) for t in range(per_group)], axis=0)
+        sums = sums + dot_nt(spread, wide_one_hot(width, lane))
     for t in range(per_group):
         at = t * 2 * fields
         tiles[t] = sums[at : at + fields] + sums[at + fields : at + 2 * fields]
@@ -169,33 +184,34 @@
     return split(tile[3:4].astype(jnp.int32), size_z)
 
 
-def scatter_kernel(size_y, ends, tiles, load):
+def scatter_kernel(size_y, slabs_of, tiles, load):
     parts, size_xy, size_z = load.shape
-    per_group = tiles.shape[0] // ends.shape[0]
+    groups = slabs_of.shape[0]
+    per_group = tiles.shape[0] // groups
+    slabs = size_xy // size_y
     half = parts * size_y
     load[...] = jnp.zeros_like(load)
 
-    def one_tile(t, carry):
-        group, index = t // per_group, t % per_group
-        tile = tiles[t]
-        xy, z = located(tile, size_z)
-        at_z = one_hot(matches(size_z, z))
-        pairs = [two_terms(tile[k : k + 1]) for k in range(parts)]
-        values = [hi for hi, lo in pairs] + [lo for hi, lo in pairs]
-
-        def one_slab(x, carry):
-            at_y = matches(size_y, xy - x * size_y)
+    def body(step, carry):
+        made = []
+        for group in range(groups):
+            slab = slabs_of[group, 0, step]
+            tile = tiles[group * per_group + jnp.minimum(step - slab, per_group - 1)]
+            xy, z = located(tile, size_z)
+            at_z = wide_one_hot(size_z, z)
+            pairs = [two_terms(tile[k : k + 1]) for k in range(parts)]
+            values = [hi for hi, lo in pairs] + [lo for hi, lo in pairs]
+            at_y = matches(size_y, xy - slab * size_y)
             terms = jnp.concatenate([scaled(at_y, value) for value in values], axis=0)
             product = dot_nt(terms, at_z)
-            product = product[:half] + product[half:]
-            span = pl.ds(pl.multiple_of(x * size_y, size_y), size_y)
+            made.append((slab, product[:half] + product[half:]))
+        for slab, product in made:
+            span = pl.ds(pl.multiple_of(jnp.minimum(slab, slabs - 1) * size_y, size_y), size_y)
             for k in range(parts):
                 load[k, span] = load[k, span] + product[k * size_y : (k + 1) * size_y]
-            return carry
-
-        return lax.fori_loop(ends[group, 0, index], ends[group, 1, index] + 1, one_slab, carry)
-
-    lax.fori_loop(0, tiles.shape[0], one_tile, 0)
+        return carry
+
+    lax.fori_loop(0, per_group + slabs, body, 0, unroll=4)
 
 
 def scatter_rows(tiles, ends, size_x, size_y, size_z):
@@ -208,13 +224,13 @@
     )(ends, tiles)
 
 
-def gather_kernel(ends, tiles, field, boxes, terms, sums):
+def gather_kernel(slabs_of, tiles, field, boxes, terms, found):
     parts, size_x, size_y, size_z = field.shape
-    per_group = tiles.shape[0] // ends.shape[0]
+    groups = slabs_of.shape[0]
+    count, _, width = tiles.shape
+    per_group = count // groups
     devices = boxes.shape[0]
     half = parts * size_y
-    width = tiles.shape[2]
-    sums[...] = jnp.zeros_like(sums)
 
     def cut(x, carry):
         for k in range(parts):
@@ -224,42 +240,50 @@
         return carry
 
     lax.fori_loop(0, size_x, cut, 0)
-
-    def one_tile(t, carry):
-        group, index = t // per_group, t % per_group
-        tile = tiles[t]
-        xy, z = located(tile, size_z)
-        at_z = one_hot(matches(size_z, z))
-
-        def one_slab(x, found):
-            at_y = matches(size_y, xy - x * size_y)
-            columns = jnp.dot(terms[x], at_z, preferred_element_type=F32)
+    found[...] = jnp.zeros_like(found)
+
+    def body(step, carry):
+        made = []
+        for group in range(groups):
+            slab = slabs_of[group, 0, step]
+            number = group * per_group + jnp.minimum(step - slab, per_group - 1)
+            tile = tiles[number]
+            xy, z = located(tile, size_z)
+            at_z = wide_one_hot(size_z, z)
+            at_y = matches(size_y, xy - slab * size_y)
+            columns = jnp.dot(terms[jnp.minimum(slab, size_x - 1)], at_z, preferred_element_type=F32)
             columns = columns[:half] + columns[half:]
-            return tuple(
-                found[k] + jnp.sum(jnp.where(at_y, columns[k * size_y : (k + 1) * size_y], 0.0).reshape(size_y // 8, 8, width), axis=0)
+            sums = [
+                jnp.sum(jnp.where(at_y, columns[k * size_y : (k + 1) * size_y], 0.0), axis=0, keepdims=True)
                 for k in range(parts)
-            )
-
-        empty = tuple(jnp.zeros((8, width), F32) for _ in range(parts))
-        found = lax.fori_loop(ends[group, 0, index], ends[group, 1, index] + 1, one_slab, empty)
-        owner, slot = split(tile[5:6].astype(jnp.int32), BOX_DEV)
+            ]
+            made.append((number, sums))
+        for number, sums in made:
+            for k in range(parts):
+                found[k, pl.ds(number, 1)] = found[k, pl.ds(number, 1)] + sums[k]
+        return carry
+
+    lax.fori_loop(0, per_group + size_x, body, 0, unroll=4)
+    total = jnp.zeros((2 * parts * devices, BOX_DEV), F32)
+    join = 8
+    for first in range(0, count, join):
+        def line(field):
+            return jnp.concatenate([tiles[t, field : field + 1] for t in range(first, first + join)], axis=1)
+        owner, slot = split(line(5).astype(jnp.int32), BOX_DEV)
+        weight = line(4)
         at_owner = matches(devices, owner)
-        pairs = [two_terms(jnp.sum(part, axis=0, keepdims=True) * tile[4:5]) for part in found]
+        pairs = [two_terms(jnp.concatenate([found[k, t : t + 1] for t in range(first, first + join)], axis=1) * weight) for k in range(parts)]
         values = [hi for hi, lo in pairs] + [lo for hi, lo in pairs]
         spread = jnp.concatenate([scaled(at_owner, value) for value in values], axis=0)
-        sums[...] = sums[...] + dot_nt(spread, one_hot(matches(BOX_DEV, slot)))
-        return carry
-
-    lax.fori_loop(0, tiles.shape[0], one_tile, 0)
+        total = total + dot_nt(spread, one_hot(matches(BOX_DEV, slot)))
     for k in range(parts):
-        part = sums[k * devices : (k + 1) * devices] + sums[(parts + k) * devices : (parts + k + 1) * devices]
+        part = total[k * devices : (k + 1) * devices] + total[(parts + k) * devices : (parts + k + 1) * devices]
         boxes[:, k * BOX_DEV : (k + 1) * BOX_DEV] = part
 
 
-def gather_rows(tiles, ends, field):
+def gather_rows(tiles, ends, field, devices):
     groups = ends.shape[0]
     parts, size_x, size_y, size_z = field.shape
-    devices = lax.axis_size("gx") * lax.axis_size("gy")
     return pl.pallas_call(
         gather_kernel,
         out_shape=jax.ShapeDtypeStruct((devices, 3 * BOX_DEV), F32),
@@ -267,7 +291,7 @@
         out_specs=pl.BlockSpec(memory_space=pltpu.VMEM),
         scratch_shapes=[
             pltpu.VMEM((size_x, 2 * parts * size_y, size_z), BF16),
-            pltpu.VMEM((2 * parts * devices, BOX_DEV), F32),
+            pltpu.VMEM((3, tiles.shape[0], tiles.shape[2]), F32),
         ],
         name="gather_rows",
     )(ends, tiles, field)
@@ -513,7 +537,7 @@
     load = scatter_rows(tiles, ends, size_x, size_y, size_z)
     load = load.reshape(3, size_x, size_y, size_z)
     adjoint = solve_sweeps(load, stiffness, anchor, coupling)
-    partial = gather_rows(tiles, ends, adjoint)
+    partial = gather_rows(tiles, ends, adjoint, devices)
     partial = exchange(partial.reshape(devices, 1, 3 * BOX_DEV), 1, 2)
     box_gradient = jnp.sum(partial, axis=(0, 1)).reshape(3, BOX_DEV)
     return (adjoint, box_gradient)

time: 144 us -> 92.4 us (0.64)
  Pallas kernels: 139 us -> 87.3 us
    pallas_call x1, Pallas kernels: 38.6 us -> 9.28 us  [gather_rows(): pl.pallas_call(gather_kernel, out_shape=jax.ShapeDtypeStruct((devices, 3...]
    pallas_call x1, Pallas kernels: 31 us -> 9.2 us  [scatter_rows(): pl.pallas_call(functools.partial(scatter_kernel, size_y), out_shape=jax.S...]
where the time goes in v2:
time: 92.4 us; the launch traced here: 91.9 us
  Pallas kernels  87.3 us (94%)
  local copies, waits for them, and re-layouts  3.19 us (3%)
    pallas_call x2, Pallas kernels, exchange(): pl.pallas_call(functools.partial(exchange_kernel, live), out_shape=jax.Sh...  26.6 us
    pallas_call x1, Pallas kernels, solve_sweeps(): pl.pallas_call(sweep_kernel, out_shape=jax.ShapeDtypeStruct(load.shape, F...  22.2 us
    pallas_call x1, Pallas kernels, pack_rows(): pl.pallas_call(functools.partial(pack_kernel, step), out_shape=jax.ShapeD...  13.3 us
    pallas_call x1, Pallas kernels, gather_rows(): pl.pallas_call(gather_kernel, out_shape=jax.ShapeDtypeStruct((devices, 3...  9.28 us
    pallas_call x1, Pallas kernels, scatter_rows(): pl.pallas_call(functools.partial(scatter_kernel, size_y), out_shape=jax.S...  9.2 us
    pallas_call x1, Pallas kernels, sort_rows(): pl.pallas_call(functools.partial(sort_kernel, cut, slabs), grid=(groups,)...  6.65 us

profile of v2, /device:TPU:0, one launch (start us, length us, event | category | flops | bytes accessed | tf_op | source)
XLA Modules:
  0.0 91.9 jit_solution(3836332625476630364)
XLA Ops:
  0.6 13.3 %pack_rows.1.send = f32[32,8,512]{2,1,0:T(8,128)} custom-call(f32[3,8192]{1,0:T(4,128)} %sens.1, f32[1,8192]{1,0:T(1,128)} %bitcast.7, s32[1,8192]{1,0:T(1,128)} %bitcast.8, s32[1,8192]{1,0:T(1,128)} %bitcast.9, s32[1,8192]{1,0:T(1,128)} %bitcast.10, s32[1,8192]{1,0:T(1,128)} %bitcast.11), custom_call_target="tpu_custom_call" | custom-call | tf_op jit(solution)/shard_map/pack_rows/pallas_call | solution.py:84
  14.0 16.3 %exchange_1.1.arrived = f32[32,8,512]{2,1,0:T(8,128)} custom-call(f32[32,8,512]{2,1,0:T(8,128)} %pack_rows.1.send), custom_call_target="tpu_custom_call" | custom-call | tf_op jit(solution)/shard_map/exchange_1/pallas_call | solution.py:493
  30.2 6.6 %sort_rows.1 = (f32[64,8,256]{2,1,0:T(8,128)}, s32[4,8,128]{2,1,0:T(8,128)}) custom-call(f32[32,8,512]{2,1,0:T(8,128)} %exchange_1.1.arrived), custom_call_target="tpu_custom_call" | custom-call | tf_op jit(solution)/shard_map/sort_rows/pallas_call | solution.py:167
  36.9 9.2 %scatter_rows.1 = f32[3,512,256]{2,1,0:T(8,128)} custom-call(s32[4,8,128]{2,1,0:T(8,128)} %get-tuple-element.4.slabs_of, f32[64,8,256]{2,1,0:T(8,128)} %get-tuple-element.5.tiles), custom_call_target="tpu_custom_call" | custom-call | tf_op jit(solution)/shard_map/scatter_rows/pallas_call | solution.py:218
  46.1 22.2 %sweeps.1.field = f32[3,16,32,256]{3,2,1,0:T(8,128)} custom-call(f32[3,16,32,256]{3,2,1,0:T(8,128)} %bitcast.6, f32[16,32,256]{2,1,0:T(8,128)} %stiff.1, f32[3,16,32,256]{3,2,1,0:T(8,128)} %anchor.1, f32[9,16,32,256]{3,2,1,0:T(8,128)} %coupling.1), custom_call_target="tpu_custom_call" | custom-call | tf_op jit(solution)/shard_map/sweeps/pallas_call | solution.py:429
  68.3 0.0 copy-start
  68.3 9.3 %gather_rows.1 = f32[32,192]{1,0:T(8,128)} custom-call(s32[4,8,128]{2,1,0:T(8,128)} %get-tuple-element.4.slabs_of, f32[64,8,256]{2,1,0:T(8,128)} %get-tuple-element.5.tiles, f32[3,16,32,256]{3,2,1,0:T(8,128)} %sweeps.1.field), custom_call_target="tpu_custom_call" | custom-call | tf_op jit(solution)/shard_map/gather_rows/pallas_call | solution.py:287
  77.6 1.4 %reshape.34.send = f32[32,1,192]{2,1,0:T(1,128)} reshape(f32[32,192]{1,0:T(8,128)} %gather_rows.1) | data formatting | bytes 49152 | tf_op jit(solution)/shard_map/reshape | solution.py:541
  79.0 10.3 %exchange_2.1 = f32[32,1,192]{2,1,0:T(1,128)} custom-call(f32[32,1,192]{2,1,0:T(1,128)} %reshape.34.send), custom_call_target="tpu_custom_call" | custom-call | tf_op jit(solution)/shard_map/exchange_2/pallas_call | solution.py:493
  89.3 0.8 reduce_sum.9
  90.1 0.7 reshape.35
  90.8 0.0 copy-done
  90.8 1.1 %copy.12 = f32[3,16,32,256]{3,2,1,0:T(8,128)} copy(f32[3,16,32,256]{3,2,1,0:T(8,128)S(1)} %copy-done) | data formatting | bytes 3145728
Async XLA Ops:
  68.3 22.5 %copy-start = (f32[3,16,32,256]{3,2,1,0:T(8,128)S(1)}, f32[3,16,32,256]{3,2,1,0:T(8,128)}, u32[]{:S(2)}) copy-start(f32[3,16,32,256]{3,2,1,0:T(8,128)} %sweeps.1.field) | copy-start | bytes 4718596

commit v3 on v2

--- a/solution.py
+++ b/solution.py
@@ -37,60 +37,6 @@
     return lax.dot_general(a, b, NT, preferred_element_type=F32)
 
 
-def pack_kernel(step, sens, weight, device, cell, owner, slot, out, tri, seen):
-    targets, fields, capacity = out.shape
-    rows = sens.shape[1]
-    out[...] = jnp.zeros_like(out)
-    seen[...] = jnp.zeros_like(seen)
-    tri[...] = one_hot(
-        lax.broadcasted_iota(jnp.int32, (step, step), 0)
-        < lax.broadcasted_iota(jnp.int32, (step, step), 1)
-    )
-
-    def block(index, carry):
-        span = pl.ds(pl.multiple_of(index * step, step), step)
-        target = device[:, span]
-        chosen = matches(targets, target)
-        before = jnp.dot(one_hot(chosen), tri[...], preferred_element_type=F32) + seen[:, :1]
-        rank = jnp.sum(jnp.where(chosen, before, 0.0), axis=0, keepdims=True).astype(jnp.int32)
-        seen[...] = seen[...] + jnp.sum(jnp.where(chosen, 1.0, 0.0), axis=1, keepdims=True)
-        place = one_hot(matches(capacity, rank))
-        payload = jnp.concatenate(
-            [
-                sens[:, span],
-                cell[:, span].astype(F32),
-                weight[:, span],
-                (owner[:, span] * BOX_DEV + slot[:, span]).astype(F32),
-                jnp.zeros((fields - SENT, step), F32),
-            ],
-            axis=0,
-        )
-        wide = (targets, fields, step)
-        to = lax.broadcasted_iota(jnp.int32, wide, 0) == target[None]
-        terms = [
-            jnp.where(to, term[None], 0.0).reshape(targets * fields, step).astype(BF16)
-            for term in two_terms(payload)
-        ]
-        product = dot_nt(jnp.concatenate(terms, axis=0), place)
-        product = product[: targets * fields] + product[targets * fields :]
-        out[...] = out[...] + product.reshape(targets, fields, capacity)
-        return carry
-
-    lax.fori_loop(0, rows // step, block, 0)
-
-
-def pack_rows(devices, capacity, sens, weight, device, cell, owner, slot):
-    step = min(2048, sens.shape[1])
-    return pl.pallas_call(
-        functools.partial(pack_kernel, step),
-        out_shape=jax.ShapeDtypeStruct((devices, 8, capacity), F32),
-        in_specs=[pl.BlockSpec(memory_space=pltpu.VMEM)] * 6,
-        out_specs=pl.BlockSpec(memory_space=pltpu.VMEM),
-        scratch_shapes=[pltpu.VMEM((step, step), BF16), pltpu.VMEM((devices, 128), F32)],
-        name="pack_rows",
-    )(sens, weight, device, cell, owner, slot)
-
-
 def split(value, size):
     if size & (size - 1) == 0:
         return value >> (size.bit_length() - 1), value & (size - 1)
@@ -109,75 +55,191 @@
     return jnp.where(mask, values, jnp.array(0, BF16))
 
 
-def sort_kernel(cut, slabs, arrived, tiles, ends):
-    senders, fields, capacity = arrived.shape
-    per_group, _, width = tiles.shape
-    join = max(1, min(senders, 512 // capacity))
-    count, length = senders // join, join * capacity
-    blocks = [
-        jnp.concatenate([arrived[q * join + i] for i in range(join)], axis=1)
-        for q in range(count)
-    ]
-    chosen = [matches(slabs, split(block[3:4].astype(jnp.int32), cut)[0]) for block in blocks]
+def running(numbers):
+    totals = [jnp.zeros_like(numbers[0])]
+    for number in numbers:
+        totals.append(totals[-1] + number)
+    return totals
+
+
+def ordinals(chosen):
+    length = chosen[0].shape[1]
     stacked = one_hot(jnp.concatenate(chosen, axis=0))
-    total = count * slabs
     earlier = one_hot(
         lax.broadcasted_iota(jnp.int32, (length, length), 0)
         < lax.broadcasted_iota(jnp.int32, (length, length), 1)
     )
     before = jnp.dot(stacked, earlier, preferred_element_type=F32)
     number = jnp.dot(stacked, jnp.ones((length, 128), BF16), preferred_element_type=F32)
-    this = lax.broadcasted_iota(jnp.int32, (total, total), 0)
-    other = lax.broadcasted_iota(jnp.int32, (total, total), 1)
-    ahead = one_hot((other % slabs < this % slabs) | ((other % slabs == this % slabs) & (other < this)))
-    tens = jnp.floor(number * 0.0625)
-    first = 16.0 * jnp.dot(ahead, tens.astype(BF16), preferred_element_type=F32)
-    first = first + jnp.dot(ahead, (number - 16.0 * tens).astype(BF16), preferred_element_type=F32)
+    size = chosen[0].shape[0]
+
+    def cut(values):
+        return [values[q * size : (q + 1) * size] for q in range(len(chosen))]
+
+    return cut(before), cut(number)
+
+
+def picked(mask, value):
+    return jnp.sum(jnp.where(mask, value, 0.0), axis=0, keepdims=True)
+
+
+def relay_kernel(cut, slabs, parts, sens, weight, device, cell, owner, slot, tiles, slab_of, send, recv, place, spread, send_sem, recv_sem):
+    count, fields, capacity = send.shape
+    rows = sens.shape[1]
+    _, _, width = tiles.shape
+    groups = slab_of.shape[0]
+    per_group = tiles.shape[0] // groups
+    gx, gy = lax.axis_index("gx"), lax.axis_index("gy")
+    size_x, size_y = lax.axis_size("gx"), lax.axis_size("gy")
+    me = gx * size_y + gy
+    barrier = pltpu.get_barrier_semaphore()
+
+    def peer(step):
+        there = (me + step) % count
+        return (there // size_y, there % size_y)
+
+    def greet(step, carry):
+        pl.semaphore_signal(barrier, inc=1, device_id=peer(step), device_id_type=MESH)
+        return carry
+
+    lax.fori_loop(1, count, greet, 0)
+
+    length = min(512, rows)
+    chunks = rows // length
+    spans = [slice(q * length, (q + 1) * length) for q in range(chunks)]
+    target = device[...] - me
+    target = jnp.where(target < 0, target + count, target)
+    chosen = [matches(count, target[:, span]) for span in spans]
+    before, number = ordinals(chosen)
+    total = running(number)
+    for q, span in enumerate(spans):
+        rank = picked(chosen[q], before[q] + total[q][:, :1]).astype(jnp.int32)
+        place[:, span] = wide_one_hot(capacity, rank)
+
+    def copy(step):
+        return pltpu.make_async_remote_copy(
+            src_ref=send.at[step, pl.ds(0, SENT)],
+            dst_ref=recv.at[step, pl.ds(0, SENT)],
+            send_sem=send_sem.at[step],
+            recv_sem=recv_sem.at[step],
+            device_id=peer(step),
+            device_id_type=MESH,
+        )
+
+    def start(step, carry):
+        copy(step).start()
+        return carry
+
+    share = count // parts
+    for part in reversed(range(parts)):
+        for q, span in enumerate(spans):
+            payload = jnp.concatenate(
+                [
+                    sens[:, span],
+                    cell[:, span].astype(F32),
+                    weight[:, span],
+                    (owner[:, span] * BOX_DEV + slot[:, span]).astype(F32),
+                    jnp.zeros((fields - SENT, length), F32),
+                ],
+                axis=0,
+            )
+            terms = jnp.concatenate(two_terms(payload), axis=0).astype(BF16)
+            to = jnp.broadcast_to(target[:, span] - part * share, terms.shape).astype(jnp.int16)
+            for t in range(share):
+                spread[t * 2 * fields : (t + 1) * 2 * fields, span] = kept(to == t, terms)
+        product = dot_nt(spread[...], place[...])
+        for t in range(share):
+            at = t * 2 * fields
+            send[part * share + t] = product[at : at + fields] + product[at + fields : at + 2 * fields]
+        if part == parts - 1:
+            pl.semaphore_wait(barrier, count - 1)
+        lax.fori_loop(max(1, part * share), (part + 1) * share, start, 0)
+
+    recv[0] = send[0]
+
+    def arrive(step, carry):
+        copy(step).wait_recv()
+        return carry
+
+    senders = count // groups
+    for group in reversed(range(groups)):
+        lax.fori_loop(max(1, group * senders), (group + 1) * senders, arrive, 0)
+        sort_group(cut, slabs, [recv.at[group * senders + i] for i in range(senders)], tiles, group * per_group, per_group, slab_of, group)
+
+    def sent(step, carry):
+        copy(step).wait_send()
+        return carry
+
+    lax.fori_loop(1, count, sent, 0)
+
+
+def sort_group(cut, slabs, arrived, tiles, first, per_group, slab_of, group):
+    senders = len(arrived)
+    fields, capacity = arrived[0].shape
+    width = tiles.shape[2]
+    join = max(1, min(senders, 512 // capacity))
+    count = senders // join
+    real = lax.broadcasted_iota(jnp.int32, (fields, join * capacity), 0) < SENT
+    blocks = [
+        jnp.where(real, jnp.concatenate([arrived[q * join + i][...] for i in range(join)], axis=1), 0.0)
+        for q in range(count)
+    ]
+    chosen = [matches(slabs, split(block[3:4].astype(jnp.int32), cut)[0]) for block in blocks]
+    before, number = ordinals(chosen)
+    total = running(number)
+    lower = one_hot(
+        lax.broadcasted_iota(jnp.int32, (slabs, slabs), 1)
+        < lax.broadcasted_iota(jnp.int32, (slabs, slabs), 0)
+    )
+    tens = jnp.floor(total[-1] * 0.0625)
+    start = 16.0 * jnp.dot(lower, tens.astype(BF16), preferred_element_type=F32)
+    start = start + jnp.dot(lower, (total[-1] - 16.0 * tens).astype(BF16), preferred_element_type=F32)
 
     steps = per_group + slabs - 1
-    start = first[:slabs]
     row = lax.broadcasted_iota(jnp.int32, start.shape, 0).astype(F32)
     step = lax.broadcasted_iota(jnp.int32, start.shape, 1).astype(F32)
     entry = row + jnp.minimum(jnp.floor(start * (1.0 / width)), per_group - 1.0)
     slab = jnp.sum(jnp.where((row > 0) & (entry <= step), 1.0, 0.0), axis=0, keepdims=True)
     slab = jnp.where(step[:1] < steps, slab, slabs)
-    ends[0] = jnp.broadcast_to(slab, (8, 128)).astype(jnp.int32)
+    slab_of[group] = jnp.broadcast_to(slab, (8, 128)).astype(jnp.int32)
 
     sums = jnp.zeros((per_group * 2 * fields, width), F32)
     for q in range(count):
-        rows = slice(q * slabs, (q + 1) * slabs)
-        where = before[rows] + first[rows, :1]
-        place = jnp.sum(jnp.where(chosen[q], where, 0.0), axis=0, keepdims=True).astype(jnp.int32)
-        tile, lane = split(place, width)
+        where = picked(chosen[q], before[q] + (total[q] + start)[:, :1]).astype(jnp.int32)
+        tile, lane = split(where, width)
         terms = jnp.concatenate(two_terms(blocks[q]), axis=0).astype(BF16)
         tile = jnp.broadcast_to(tile, terms.shape).astype(jnp.int16)
         spread = jnp.concatenate([kept(tile == t, terms) for t in range(per_group)], axis=0)
         sums = sums + dot_nt(spread, wide_one_hot(width, lane))
     for t in range(per_group):
         at = t * 2 * fields
-        tiles[t] = sums[at : at + fields] + sums[at + fields : at + 2 * fields]
-
-
-def sort_rows(arrived, slabs, cut):
-    devices, fields, capacity = arrived.shape
+        tiles[first + t] = sums[at : at + fields] + sums[at + fields : at + 2 * fields]
+
+
+def relay_rows(devices, capacity, slabs, cut, sens, weight, device, cell, owner, slot):
     rows = devices * capacity
     size = min(4096, rows)
     width = min(256, size)
     groups = rows // size
+    parts = 2
     return pl.pallas_call(
-        functools.partial(sort_kernel, cut, slabs),
-        grid=(groups,),
+        functools.partial(relay_kernel, cut, slabs, parts),
         out_shape=[
-            jax.ShapeDtypeStruct((rows // width, fields, width), F32),
+            jax.ShapeDtypeStruct((rows // width, 8, width), F32),
             jax.ShapeDtypeStruct((groups, 8, 128), jnp.int32),
         ],
-        in_specs=[pl.BlockSpec((size // capacity, fields, capacity), lambda i: (i, 0, 0))],
-        out_specs=[
-            pl.BlockSpec((size // width, fields, width), lambda i: (i, 0, 0)),
-            pl.BlockSpec((1, 8, 128), lambda i: (i, 0, 0)),
-        ],
-        name="sort_rows",
-    )(arrived)
+        in_specs=[pl.BlockSpec(memory_space=pltpu.VMEM)] * 6,
+        out_specs=[pl.BlockSpec(memory_space=pltpu.VMEM)] * 2,
+        scratch_shapes=[
+            pltpu.VMEM((devices, 8, capacity), F32),
+            pltpu.VMEM((devices, 8, capacity), F32),
+            pltpu.VMEM((capacity, sens.shape[1]), BF16),
+            pltpu.VMEM((devices // parts * 16, sens.shape[1]), BF16),
+        ]
+        + [pltpu.SemaphoreType.DMA((devices,))] * 2,
+        compiler_params=pltpu.CompilerParams(collective_id=1, has_side_effects=True),
+        name="relay_rows",
+    )(sens, weight, device, cell, owner, slot)
 
 
 def located(tile, size_z):
@@ -522,9 +584,11 @@
     def row(values):
         return values.reshape(1, row_count)
 
-    packed = pack_rows(
+    tiles, ends = relay_rows(
         devices,
         capacity,
+        size_x,
+        size_y * size_z,
         sensitivity,
         row(node_weight),
         row(dest_device),
@@ -532,8 +596,6 @@
         row(box_owner),
         row(box_slot),
     )
-    arrived = exchange(packed, SENT, 1)
-    tiles, ends = sort_rows(arrived, size_x, size_y * size_z)
     load = scatter_rows(tiles, ends, size_x, size_y, size_z)
     load = load.reshape(3, size_x, size_y, size_z)
     adjoint = solve_sweeps(load, stiffness, anchor, coupling)

time: 92.4 us -> 79.2 us (0.86)
  Pallas kernels: 87.3 us -> 74.2 us
    pallas_call x2 -> x1, Pallas kernels: 26.6 us -> 10.6 us  [exchange(): pl.pallas_call(functools.partial(exchange_kernel, live), out_shape=jax.Sh...]
    pallas_call x2 -> x1, Pallas kernels: 20 us -> 24 us  [relay_rows(): pl.pallas_call(functools.partial(relay_kernel, cut, slabs, parts), out_sh...]
    pallas_call x1, Pallas kernels: 22.2 us -> 21.1 us  [solve_sweeps(): pl.pallas_call(sweep_kernel, out_shape=jax.ShapeDtypeStruct(load.shape, F...]
where the time goes in v3:
time: 79.2 us; the launch traced here: 78.9 us
  Pallas kernels  74.2 us (94%)
  local copies, waits for them, and re-layouts  3.19 us (4%)
  other arithmetic  0.81 us (1%)
    pallas_call x1, Pallas kernels, relay_rows(): pl.pallas_call(functools.partial(relay_kernel, cut, slabs, parts), out_sh...  24 us
    pallas_call x1, Pallas kernels, solve_sweeps(): pl.pallas_call(sweep_kernel, out_shape=jax.ShapeDtypeStruct(load.shape, F...  21.1 us
    pallas_call x1, Pallas kernels, exchange(): pl.pallas_call(functools.partial(exchange_kernel, live), out_shape=jax.Sh...  10.6 us
    pallas_call x1, Pallas kernels, gather_rows(): pl.pallas_call(gather_kernel, out_shape=jax.ShapeDtypeStruct((devices, 3...  9.28 us
    pallas_call x1, Pallas kernels, scatter_rows(): pl.pallas_call(functools.partial(scatter_kernel, size_y), out_shape=jax.S...  9.2 us

profile of v3, /device:TPU:0, one launch (start us, length us, event | category | flops | bytes accessed | tf_op | source)
XLA Modules:
  0.0 78.9 jit_solution(13088960945579980759)
XLA Ops:
  0.6 24.0 %relay_rows.1 = (f32[64,8,256]{2,1,0:T(8,128)}, s32[4,8,128]{2,1,0:T(8,128)}) custom-call(f32[3,8192]{1,0:T(4,128)} %sens.1, f32[1,8192]{1,0:T(1,128)} %bitcast.7, s32[1,8192]{1,0:T(1,128)} %bitcast.8, s32[1,8192]{1,0:T(1,128)} %bitcast.9, s32[1,8192]{1,0:T(1,128)} %bitcast.10, s32[1,8192]{1,0:T(1,128)} %bitcast.11), custom_call_target="tpu_custom_call" | custom-call | tf_op jit(solution)/shard_map/relay_rows/pallas_call | solution.py:225
  24.6 9.2 %scatter_rows.1 = f32[3,512,256]{2,1,0:T(8,128)} custom-call(s32[4,8,128]{2,1,0:T(8,128)} %get-tuple-element.4.slabs_of, f32[64,8,256]{2,1,0:T(8,128)} %get-tuple-element.5.tiles), custom_call_target="tpu_custom_call" | custom-call | tf_op jit(solution)/shard_map/scatter_rows/pallas_call | solution.py:280
  33.8 21.1 %sweeps.1.field = f32[3,16,32,256]{3,2,1,0:T(8,128)} custom-call(f32[3,16,32,256]{3,2,1,0:T(8,128)} %bitcast.6, f32[16,32,256]{2,1,0:T(8,128)} %stiff.1, f32[3,16,32,256]{3,2,1,0:T(8,128)} %anchor.1, f32[9,16,32,256]{3,2,1,0:T(8,128)} %coupling.1), custom_call_target="tpu_custom_call" | custom-call | tf_op jit(solution)/shard_map/sweeps/pallas_call | solution.py:491
  54.9 0.0 copy-start
  54.9 9.3 %gather_rows.1 = f32[32,192]{1,0:T(8,128)} custom-call(s32[4,8,128]{2,1,0:T(8,128)} %get-tuple-element.4.slabs_of, f32[64,8,256]{2,1,0:T(8,128)} %get-tuple-element.5.tiles, f32[3,16,32,256]{3,2,1,0:T(8,128)} %sweeps.1.field), custom_call_target="tpu_custom_call" | custom-call | tf_op jit(solution)/shard_map/gather_rows/pallas_call | solution.py:349
  64.2 1.4 %reshape.34.send = f32[32,1,192]{2,1,0:T(1,128)} reshape(f32[32,192]{1,0:T(8,128)} %gather_rows.1) | data formatting | bytes 49152 | tf_op jit(solution)/shard_map/reshape | solution.py:603
  65.6 10.6 %exchange_2.1 = f32[32,1,192]{2,1,0:T(1,128)} custom-call(f32[32,1,192]{2,1,0:T(1,128)} %reshape.34.send), custom_call_target="tpu_custom_call" | custom-call | tf_op jit(solution)/shard_map/exchange_2/pallas_call | solution.py:555
  76.2 0.8 %reduce_sum.9 = f32[192]{0:T(256)S(1)} reduce(f32[32,1,192]{2,1,0:T(1,128)} %exchange_2.1, f32[]{:T(128)} %constant.0.clone.1), dimensions={0,1}, to_apply=%region_0.0 | reduce | flops 5952 | bytes 25348 | tf_op jit(solution)/shard_map/reduce_sum | solution.py:604
  77.0 0.7 reshape.35
  77.7 0.0 copy-done
  77.7 1.1 %copy.12 = f32[3,16,32,256]{3,2,1,0:T(8,128)} copy(f32[3,16,32,256]{3,2,1,0:T(8,128)S(1)} %copy-done) | data formatting | bytes 3145728
Async XLA Ops:
  54.9 22.8 %copy-start = (f32[3,16,32,256]{3,2,1,0:T(8,128)S(1)}, f32[3,16,32,256]{3,2,1,0:T(8,128)}, u32[]{:S(2)}) copy-start(f32[3,16,32,256]{3,2,1,0:T(8,128)} %sweeps.1.field) | copy-start | bytes 4718596

commit v4 on v3

--- a/solution.py
+++ b/solution.py
@@ -201,7 +201,10 @@
     entry = row + jnp.minimum(jnp.floor(start * (1.0 / width)), per_group - 1.0)
     slab = jnp.sum(jnp.where((row > 0) & (entry <= step), 1.0, 0.0), axis=0, keepdims=True)
     slab = jnp.where(step[:1] < steps, slab, slabs)
-    slab_of[group] = jnp.broadcast_to(slab, (8, 128)).astype(jnp.int32)
+    inside = (row > 0) & (start < (step + 1.0) * width)
+    final = step[:1] + jnp.sum(jnp.where(inside, 1.0, 0.0), axis=0, keepdims=True)
+    table = jnp.concatenate([slab, final, jnp.zeros((6, 128), F32)], axis=0)
+    slab_of[group] = table.astype(jnp.int32)
 
     sums = jnp.zeros((per_group * 2 * fields, width), F32)
     for q in range(count):
@@ -237,7 +240,7 @@
             pltpu.VMEM((devices // parts * 16, sens.shape[1]), BF16),
         ]
         + [pltpu.SemaphoreType.DMA((devices,))] * 2,
-        compiler_params=pltpu.CompilerParams(collective_id=1, has_side_effects=True),
+        compiler_params=pltpu.CompilerParams(collective_id=1, has_side_effects=True, vmem_limit_bytes=48 << 20),
         name="relay_rows",
     )(sens, weight, device, cell, owner, slot)
 
@@ -282,175 +285,111 @@
         out_shape=jax.ShapeDtypeStruct((3, size_x * size_y, size_z), F32),
         in_specs=[pl.BlockSpec(memory_space=pltpu.SMEM), pl.BlockSpec(memory_space=pltpu.VMEM)],
         out_specs=pl.BlockSpec(memory_space=pltpu.VMEM),
+        compiler_params=pltpu.CompilerParams(vmem_limit_bytes=32 << 20),
         name="scatter_rows",
     )(ends, tiles)
 
 
-def gather_kernel(slabs_of, tiles, field, boxes, terms, found):
-    parts, size_x, size_y, size_z = field.shape
-    groups = slabs_of.shape[0]
-    count, _, width = tiles.shape
-    per_group = count // groups
-    devices = boxes.shape[0]
-    half = parts * size_y
-
-    def cut(x, carry):
-        for k in range(parts):
-            hi, lo = two_terms(field[k, x])
-            terms[x, k * size_y : (k + 1) * size_y] = hi.astype(BF16)
-            terms[x, half + k * size_y : half + (k + 1) * size_y] = lo.astype(BF16)
-        return carry
-
-    lax.fori_loop(0, size_x, cut, 0)
-    found[...] = jnp.zeros_like(found)
-
-    def body(step, carry):
-        made = []
-        for group in range(groups):
-            slab = slabs_of[group, 0, step]
-            number = group * per_group + jnp.minimum(step - slab, per_group - 1)
-            tile = tiles[number]
-            xy, z = located(tile, size_z)
-            at_z = wide_one_hot(size_z, z)
-            at_y = matches(size_y, xy - slab * size_y)
-            columns = jnp.dot(terms[jnp.minimum(slab, size_x - 1)], at_z, preferred_element_type=F32)
-            columns = columns[:half] + columns[half:]
-            sums = [
-                jnp.sum(jnp.where(at_y, columns[k * size_y : (k + 1) * size_y], 0.0), axis=0, keepdims=True)
-                for k in range(parts)
-            ]
-            made.append((number, sums))
-        for number, sums in made:
-            for k in range(parts):
-                found[k, pl.ds(number, 1)] = found[k, pl.ds(number, 1)] + sums[k]
-        return carry
-
-    lax.fori_loop(0, per_group + size_x, body, 0, unroll=4)
-    total = jnp.zeros((2 * parts * devices, BOX_DEV), F32)
-    join = 8
-    for first in range(0, count, join):
-        def line(field):
-            return jnp.concatenate([tiles[t, field : field + 1] for t in range(first, first + join)], axis=1)
-        owner, slot = split(line(5).astype(jnp.int32), BOX_DEV)
-        weight = line(4)
-        at_owner = matches(devices, owner)
-        pairs = [two_terms(jnp.concatenate([found[k, t : t + 1] for t in range(first, first + join)], axis=1) * weight) for k in range(parts)]
-        values = [hi for hi, lo in pairs] + [lo for hi, lo in pairs]
-        spread = jnp.concatenate([scaled(at_owner, value) for value in values], axis=0)
-        total = total + dot_nt(spread, one_hot(matches(BOX_DEV, slot)))
-    for k in range(parts):
-        part = total[k * devices : (k + 1) * devices] + total[(parts + k) * devices : (parts + k + 1) * devices]
-        boxes[:, k * BOX_DEV : (k + 1) * BOX_DEV] = part
-
-
-def gather_rows(tiles, ends, field, devices):
-    groups = ends.shape[0]
-    parts, size_x, size_y, size_z = field.shape
-    return pl.pallas_call(
-        gather_kernel,
-        out_shape=jax.ShapeDtypeStruct((devices, 3 * BOX_DEV), F32),
-        in_specs=[pl.BlockSpec(memory_space=pltpu.SMEM)] + [pl.BlockSpec(memory_space=pltpu.VMEM)] * 2,
-        out_specs=pl.BlockSpec(memory_space=pltpu.VMEM),
-        scratch_shapes=[
-            pltpu.VMEM((size_x, 2 * parts * size_y, size_z), BF16),
-            pltpu.VMEM((3, tiles.shape[0], tiles.shape[2]), F32),
-        ],
-        name="gather_rows",
-    )(ends, tiles, field)
-
-
-def sweep_kernel(load, stiff, anchor, coupling, adjoint, weighted, rest, inverse, edge, halo, x_send, x_recv, y_send, y_recv):
+def solve_kernel(slab_of, tiles, load, stiff, anchor, coupling, adjoint, box, weighted, inverse, near, edge, halo, terms, found, flat, landed, x_send, x_recv, y_send, y_recv, box_send, box_recv):
     parts, size_x, size_y, size_z = load.shape
     exchanges = weighted.shape[0]
     gx, gy = lax.axis_index("gx"), lax.axis_index("gy")
-    last_x, last_y = lax.axis_size("gx") - 1, lax.axis_size("gy") - 1
-    sides = (("gx", gx, -1, gx > 0), ("gx", gx, 1, gx < last_x), ("gy", gy, -1, gy > 0), ("gy", gy, 1, gy < last_y))
+    count_x, count_y = lax.axis_size("gx"), lax.axis_size("gy")
+    devices = count_x * count_y
+    me = gx * count_y + gy
+    sides = (("gx", gx, -1, gx > 0), ("gx", gx, 1, gx < count_x - 1), ("gy", gy, -1, gy > 0), ("gy", gy, 1, gy < count_y - 1))
     y_at = lax.broadcasted_iota(jnp.int32, (size_y, size_z), 0)
     z_at = lax.broadcasted_iota(jnp.int32, (size_y, size_z), 1)
-
-    for index in range(exchanges):
-        for k in range(parts):
-            weighted[index, k, 0] = jnp.zeros((size_y, size_z), F32)
-            weighted[index, k, size_x + 1] = jnp.zeros((size_y, size_z), F32)
-    halo[...] = jnp.zeros_like(halo)
-
     barrier = pltpu.get_barrier_semaphore()
-    known = 0
-    for axis, place, move, present in sides:
-        known = known + present.astype(jnp.int32)
-
-        @pl.when(present)
+
+    def peer(step):
+        there = (me + step) % devices
+        return (there // count_y, there % count_y)
+
+    def greet(step, carry):
+        pl.semaphore_signal(barrier, inc=1, device_id=peer(step), device_id_type=MESH)
+        return carry
+
+    lax.fori_loop(1, devices, greet, 0)
+
+    for side, (axis, place, move, present) in enumerate(sides):
+
+        @pl.when(jnp.logical_not(present))
         def _():
-            pl.semaphore_signal(barrier, inc=1, device_id={axis: place + move}, device_id_type=MESH)
-
-    pl.semaphore_wait(barrier, known)
-
-    def copies(index):
+            for index in range(exchanges):
+                if axis == "gx":
+                    for k in range(parts):
+                        weighted[index, k, 0 if move < 0 else size_x + 1] = jnp.zeros((size_y, size_z), F32)
+                else:
+                    halo[index, side % 2] = jnp.zeros(halo.shape[2:], F32)
+
+    def transfers(index, sending, which=range(4)):
         made = []
-        for side, (axis, place, move, present) in enumerate(sides):
+        for side in which:
+            axis, place, move, present = sides[side]
             there = 1 - side % 2
+            landing = there if sending else side % 2
             if axis == "gx":
-                pair = (weighted.at[index, :, 1 if move < 0 else size_x], weighted.at[index, :, size_x + 1 if move < 0 else 0])
+                into = size_x + 1 if (move < 0) == sending else 0
+                pair = (weighted.at[index, :, 1 if move < 0 else size_x], weighted.at[index, :, into])
                 sems = (x_send, x_recv)
             else:
-                pair = (edge.at[index, side % 2], halo.at[index, there])
+                pair = (edge.at[index, side % 2], halo.at[index, landing])
                 sems = (y_send, y_recv)
             made.append((present, pltpu.make_async_remote_copy(
                 src_ref=pair[0],
                 dst_ref=pair[1],
                 send_sem=sems[0].at[index, side % 2],
-                recv_sem=sems[1].at[index, there],
+                recv_sem=sems[1].at[index, landing],
                 device_id={axis: place + move},
                 device_id_type=MESH,
             )))
         return made
 
-    def arrivals(index):
-        made = []
-        for side, (axis, place, move, present) in enumerate(sides):
-            if axis == "gx":
-                pair = (weighted.at[index, :, 1 if move < 0 else size_x], weighted.at[index, :, 0 if move < 0 else size_x + 1])
-                sems = (x_send, x_recv)
-            else:
-                pair = (edge.at[index, side % 2], halo.at[index, side % 2])
-                sems = (y_send, y_recv)
-            made.append((present, pltpu.make_async_remote_copy(
-                src_ref=pair[0],
-                dst_ref=pair[1],
-                send_sem=sems[0].at[index, side % 2],
-                recv_sem=sems[1].at[index, side % 2],
-                device_id={axis: place + move},
-                device_id_type=MESH,
-            )))
-        return made
-
-    def publish(index, x, k, value):
-        adjoint[k, x] = value
-        if index < exchanges:
-            product = stiff[x] * value
-            weighted[index, k, x + 1] = product
-            edge[index, 0, k, pl.ds(x, 1), :] = product[0:1]
-            edge[index, 1, k, pl.ds(x, 1), :] = product[size_y - 1 : size_y]
-
-    def first(x, carry):
-        for k in range(parts):
-            inverse[k, x] = 1.0 / (6.0 * stiff[x] + anchor[k, x] + coupling[4 * k, x])
-            publish(0, x, k, load[k, x] * inverse[k, x])
-        return carry
-
-    lax.fori_loop(0, size_x, first, 0)
-    for index in range(exchanges):
-        for present, copy in copies(index):
+    def begin(index):
+        for present, copy in transfers(index, True):
 
             @pl.when(present)
             def _():
                 copy.start()
 
-        def near(x, carry):
+    def arrive(index, which):
+        for present, copy in transfers(index, False, which):
+
+            @pl.when(present)
+            def _():
+                copy.wait_recv()
+
+    rims = (0, size_y - 1)
+
+    def first(x, carry):
+        stiffness = stiff[x]
+        for side, rim in enumerate(rims):
+            near[2, side, 0, pl.ds(x, 1), :] = stiffness[rim : rim + 1]
+        for k in range(parts):
+            inverted = 1.0 / (6.0 * stiffness + anchor[k, x] + coupling[4 * k, x])
+            inverse[k, x] = inverted
+            value = load[k, x] * inverted
+            adjoint[k, x] = value
+            product = stiffness * value
+            weighted[0, k, x + 1] = product
+            for side, rim in enumerate(rims):
+                near[1, side, k, pl.ds(x, 1), :] = inverted[rim : rim + 1]
+                edge[0, side, k, pl.ds(x, 1), :] = product[rim : rim + 1]
+        return carry
+
+    lax.fori_loop(0, size_x, first, 0)
+    pl.semaphore_wait(barrier, devices - 1)
+    begin(0)
+
+    for index in range(exchanges):
+        last = index + 1 == exchanges
+
+        def update(x, carry):
             fields = [adjoint[k, x] for k in range(parts)]
             for k in range(parts):
                 product = weighted[index, k, x + 1]
-                value = load[k, x]
+                value = load[k, x] + weighted[index, k, x] + weighted[index, k, x + 2]
                 for j in range(parts):
                     if j != k:
                         value = value - coupling[3 * j + k, x] * fields[j]
@@ -458,109 +397,154 @@
                 value = value + jnp.where(z_at == size_z - 1, 0.0, pltpu.roll(product, size_z - 1, 1))
                 value = value + jnp.where(y_at == 0, 0.0, pltpu.roll(product, 1, 0))
                 value = value + jnp.where(y_at == size_y - 1, 0.0, pltpu.roll(product, size_y - 1, 0))
-                rest[k, x] = value
+                value = value * inverse[k, x]
+                adjoint[k, x] = value
+                for side, rim in enumerate(rims):
+                    near[0, side, k, pl.ds(x, 1), :] = value[rim : rim + 1]
+                if not last:
+                    weighted[index + 1, k, x + 1] = stiff[x] * value
             return carry
 
-        lax.fori_loop(0, size_x, near, 0)
-        for present, copy in arrivals(index):
-
-            @pl.when(present)
-            def _():
-                copy.wait_recv()
-
-        def far(x, carry):
+        lax.fori_loop(1, size_x - 1, update, 0)
+        arrive(index, (0, 1))
+        update(0, 0)
+        update(size_x - 1, 0)
+        arrive(index, (2, 3))
+        for side, rim in enumerate(rims):
             for k in range(parts):
-                value = rest[k, x] + weighted[index, k, x] + weighted[index, k, x + 2]
-                value = value + jnp.where(y_at == 0, halo[index, 0, k, pl.ds(x, 1), :], 0.0)
-                value = value + jnp.where(y_at == size_y - 1, halo[index, 1, k, pl.ds(x, 1), :], 0.0)
-                publish(index + 1, x, k, value * inverse[k, x])
-            return carry
-
-        lax.fori_loop(0, size_x, far, 0)
+                value = near[0, side, k] + halo[index, side, k] * near[1, side, k]
+                for x in range(size_x):
+                    adjoint[k, x, rim : rim + 1, :] = value[x : x + 1]
+                if not last:
+                    product = near[2, side, 0] * value
+                    edge[index + 1, side, k] = product
+                    for x in range(size_x):
+                        weighted[index + 1, k, x + 1, rim : rim + 1, :] = product[x : x + 1]
+        if not last:
+            begin(index + 1)
+
+    count, _, width = tiles.shape
+    groups = slab_of.shape[0]
+    per_group = count // groups
+    steps = per_group + size_x
+    half = parts * size_y
+
+    def cut(x, carry):
+        for k in range(parts):
+            hi, lo = two_terms(adjoint[k, x])
+            terms[x, k * size_y : (k + 1) * size_y] = hi.astype(BF16)
+            terms[x, half + k * size_y : half + (k + 1) * size_y] = lo.astype(BF16)
+        return carry
+
+    lax.fori_loop(0, size_x, cut, 0)
+
+    def look(step, carry):
+        made = []
+        for group in range(groups):
+            held, before = carry[group]
+            slab = slab_of[group, 0, step]
+            tile = tiles[group * per_group + jnp.minimum(step - slab, per_group - 1)]
+            xy, z = located(tile, size_z)
+            at_y = matches(size_y, xy - slab * size_y)
+            columns = jnp.dot(terms[jnp.minimum(slab, size_x - 1)], wide_one_hot(size_z, z), preferred_element_type=F32)
+            columns = columns[:half] + columns[half:]
+            value = jnp.concatenate(
+                [picked(at_y, columns[k * size_y : (k + 1) * size_y]) for k in range(parts)], axis=0
+            )
+            held = value + jnp.where(slab == before, 0.0, held)
+            found[group * steps + step, :parts] = held
+            made.append((held, slab))
+        return tuple(made)
+
+    lax.fori_loop(
+        0, steps, look, tuple((jnp.zeros((parts, width), F32), jnp.int32(0)) for _ in range(groups)), unroll=4
+    )
+    total = jnp.zeros((2 * parts * devices, BOX_DEV), F32)
+    join = min(8, count)
+    for begin_at in range(0, count, join):
+        numbers = range(begin_at, begin_at + join)
+
+        def line(field):
+            return jnp.concatenate([tiles[t, field : field + 1] for t in numbers], axis=1)
+
+        owner, slot = split(line(5).astype(jnp.int32), BOX_DEV)
+        rows = jnp.concatenate(
+            [found[t // per_group * steps + slab_of[t // per_group, 1, t % per_group]][:parts] for t in numbers], axis=1
+        ) * line(4)
+        at_owner = matches(devices, owner)
+        pairs = [two_terms(rows[k : k + 1]) for k in range(parts)]
+        values = [hi for hi, lo in pairs] + [lo for hi, lo in pairs]
+        spread = jnp.concatenate([scaled(at_owner, value) for value in values], axis=0)
+        total = total + dot_nt(spread, wide_one_hot(BOX_DEV, slot))
+    for k in range(parts):
+        part = total[k * devices : (k + 1) * devices] + total[(parts + k) * devices : (parts + k + 1) * devices]
+        flat[k] = jnp.concatenate([part, jnp.zeros_like(part)], axis=1)
+
+    def parcel(step):
+        return pltpu.make_async_remote_copy(
+            src_ref=flat.at[:, pl.ds((me + step) % devices, 1)],
+            dst_ref=landed.at[:, pl.ds(step, 1)],
+            send_sem=box_send.at[step],
+            recv_sem=box_recv.at[step],
+            device_id=peer(step),
+            device_id_type=MESH,
+        )
+
+    def post(step, carry):
+        parcel(step).start()
+        return carry
+
+    lax.fori_loop(1, devices, post, 0)
+    landed[:, 0:1] = flat[:, pl.ds(me, 1)]
+
+    def collect(step, carry):
+        parcel(step).wait_recv()
+        return carry
+
+    lax.fori_loop(1, devices, collect, 0)
+    for k in range(parts):
+        box[k : k + 1] = jnp.sum(landed[k], axis=0, keepdims=True)[:, :BOX_DEV]
+
+    def sent(step, carry):
+        parcel(step).wait_send()
+        return carry
+
+    lax.fori_loop(1, devices, sent, 0)
     for index in range(exchanges):
-        for present, copy in copies(index):
+        for present, copy in transfers(index, True):
 
             @pl.when(present)
             def _():
                 copy.wait_send()
 
 
-def solve_sweeps(load, stiffness, anchor, coupling):
+def solve_rows(devices, tiles, slab_of, load, stiffness, anchor, coupling):
     parts, size_x, size_y, size_z = load.shape
     exchanges = SWEEPS - 1
+    count, fields, width = tiles.shape
+    groups = slab_of.shape[0]
+    steps = count // groups + size_x
     return pl.pallas_call(
-        sweep_kernel,
-        out_shape=jax.ShapeDtypeStruct(load.shape, F32),
-        in_specs=[pl.BlockSpec(memory_space=pltpu.VMEM)] * 4,
-        out_specs=pl.BlockSpec(memory_space=pltpu.VMEM),
+        solve_kernel,
+        out_shape=[jax.ShapeDtypeStruct(load.shape, F32), jax.ShapeDtypeStruct((parts, BOX_DEV), F32)],
+        in_specs=[pl.BlockSpec(memory_space=pltpu.SMEM)] + [pl.BlockSpec(memory_space=pltpu.VMEM)] * 5,
+        out_specs=[pl.BlockSpec(memory_space=pltpu.VMEM)] * 2,
         scratch_shapes=[
             pltpu.VMEM((exchanges, parts, size_x + 2, size_y, size_z), F32),
             pltpu.VMEM(load.shape, F32),
-            pltpu.VMEM(load.shape, F32),
+            pltpu.VMEM((3, 2, parts, size_x, size_z), F32),
             pltpu.VMEM((exchanges, 2, parts, size_x, size_z), F32),
             pltpu.VMEM((exchanges, 2, parts, size_x, size_z), F32),
+            pltpu.VMEM((size_x, 2 * parts * size_y, size_z), BF16),
+            pltpu.VMEM((groups * steps, fields, width), F32),
+            pltpu.VMEM((parts, devices, 2 * BOX_DEV), F32),
+            pltpu.VMEM((parts, devices, 2 * BOX_DEV), F32),
         ]
-        + [pltpu.SemaphoreType.DMA((exchanges, 2))] * 4,
-        compiler_params=pltpu.CompilerParams(collective_id=0, has_side_effects=True),
-        name="sweeps",
-    )(load, stiffness, anchor, coupling)
-
-
-def exchange_kernel(live, send, recv, send_sem, recv_sem, own_sem):
-    count = send.shape[0]
-    width = lax.axis_size("gy")
-    me = lax.axis_index("gx") * width + lax.axis_index("gy")
-    barrier = pltpu.get_barrier_semaphore()
-
-    def device(index):
-        return (index // width, index % width)
-
-    def greet(step, carry):
-        pl.semaphore_signal(barrier, inc=1, device_id=device((me + step) % count), device_id_type=MESH)
-        return carry
-
-    lax.fori_loop(1, count, greet, 0)
-    pl.semaphore_wait(barrier, count - 1)
-
-    def copy(step, source, landing):
-        peer = (me + step) % count
-        return pltpu.make_async_remote_copy(
-            src_ref=send.at[source, pl.ds(0, live)],
-            dst_ref=recv.at[landing, pl.ds(0, live)],
-            send_sem=send_sem.at[step],
-            recv_sem=recv_sem.at[step],
-            device_id=device(peer),
-            device_id_type=MESH,
-        )
-
-    def start(step, carry):
-        copy(step, (me + step) % count, me).start()
-        return carry
-
-    lax.fori_loop(1, count, start, 0)
-    own = pltpu.make_async_copy(send.at[me, pl.ds(0, live)], recv.at[me, pl.ds(0, live)], own_sem)
-    own.start()
-
-    def finish(step, carry):
-        copy(step, (me + step) % count, (me + count - step) % count).wait_recv()
-        copy(step, (me + step) % count, me).wait_send()
-        return carry
-
-    lax.fori_loop(1, count, finish, 0)
-    own.wait()
-
-
-def exchange(blocks, live, number):
-    count = blocks.shape[0]
-    return pl.pallas_call(
-        functools.partial(exchange_kernel, live),
-        out_shape=jax.ShapeDtypeStruct(blocks.shape, F32),
-        in_specs=[pl.BlockSpec(memory_space=pltpu.VMEM)],
-        out_specs=pl.BlockSpec(memory_space=pltpu.VMEM),
-        scratch_shapes=[pltpu.SemaphoreType.DMA((count,))] * 2 + [pltpu.SemaphoreType.DMA],
-        compiler_params=pltpu.CompilerParams(collective_id=number, has_side_effects=True),
-        name="exchange_" + str(number),
-    )(blocks)
+        + [pltpu.SemaphoreType.DMA((exchanges, 2))] * 4
+        + [pltpu.SemaphoreType.DMA((devices,))] * 2,
+        compiler_params=pltpu.CompilerParams(collective_id=0, has_side_effects=True, vmem_limit_bytes=48 << 20),
+        name="solve_rows",
+    )(slab_of, tiles, load, stiffness, anchor, coupling)
 
 
 def body(
@@ -598,10 +582,7 @@
     )
     load = scatter_rows(tiles, ends, size_x, size_y, size_z)
     load = load.reshape(3, size_x, size_y, size_z)
-    adjoint = solve_sweeps(load, stiffness, anchor, coupling)
-    partial = gather_rows(tiles, ends, adjoint, devices)
-    partial = exchange(partial.reshape(devices, 1, 3 * BOX_DEV), 1, 2)
-    box_gradient = jnp.sum(partial, axis=(0, 1)).reshape(3, BOX_DEV)
+    adjoint, box_gradient = solve_rows(devices, tiles, ends, load, stiffness, anchor, coupling)
     return (adjoint, box_gradient)
 
 

time: 79.2 us -> 69.9 us (0.88)
  Pallas kernels: 74.2 us -> 62.2 us
  local copies, waits for them, and re-layouts: 3.19 us -> 6.56 us
  other arithmetic: 0.81 us -> 0 us
    pallas_call x3 -> x1, Pallas kernels: 41 us -> 32.2 us  [solve_rows(): pl.pallas_call(solve_kernel, out_shape=[jax.ShapeDtypeStruct(load.shape,...]
    unnamed x3 -> x18, local copies, waits for them, and re-layouts: 1.15 us -> 6.56 us
    reshape x2 -> x0, local copies, waits for them, and re-layouts: 2.04 us -> none  [the longest x1 1.38 us: body(): partial = exchange(partial.reshape(devices, 1, 3 * BOX_DEV), 1, 2)]
    pallas_call x1, Pallas kernels: 24 us -> 22.2 us  [relay_rows(): pl.pallas_call(functools.partial(relay_kernel, cut, slabs, parts), out_sh...]
    pallas_call x1, Pallas kernels: 9.2 us -> 7.8 us  [scatter_rows(): pl.pallas_call(functools.partial(scatter_kernel, size_y), out_shape=jax.S...]
    reduce_sum x1 -> x0, other arithmetic: 0.81 us -> none  [body(): box_gradient = jnp.sum(partial, axis=(0, 1)).reshape(3, BOX_DEV)]
where the time goes in v4:
time: 69.9 us; the launch traced here: 69.5 us
  Pallas kernels  62.2 us (89%)
  local copies, waits for them, and re-layouts  6.56 us (9%)
  between operations  0.7 us (1%)
    pallas_call x1, Pallas kernels, solve_rows(): pl.pallas_call(solve_kernel, out_shape=[jax.ShapeDtypeStruct(load.shape,...  32.2 us
    pallas_call x1, Pallas kernels, relay_rows(): pl.pallas_call(functools.partial(relay_kernel, cut, slabs, parts), out_sh...  22.2 us
    pallas_call x1, Pallas kernels, scatter_rows(): pl.pallas_call(functools.partial(scatter_kernel, size_y), out_shape=jax.S...  7.8 us
    unnamed x18, local copies, waits for them, and re-layouts  6.56 us

profile of v4, /device:TPU:0, one launch (start us, length us, event | category | flops | bytes accessed | tf_op | source)
XLA Modules:
  0.0 69.5 jit_solution(16331795464140911545)
XLA Ops:
  0.6 0.0 copy-start
  0.6 0.0 copy-start.1
  0.7 0.0 copy-start.2
  0.7 1.0 %copy-done.2 = f32[3,8192]{1,0:T(4,128)S(1)} copy-done((f32[3,8192]{1,0:T(4,128)S(1)}, f32[3,8192]{1,0:T(4,128)}, u32[]{:S(2)}) %copy-start.2) | copy-done | bytes 98328
  1.7 0.0 copy-start.3
  1.7 0.8 %copy-done.3 = f32[8192]{0:T(1024)S(1)} copy-done((f32[8192]{0:T(1024)S(1)}, f32[8192]{0:T(1024)}, u32[]{:S(2)}) %copy-start.3) | copy-done | bytes 32792
  2.5 0.0 copy-start.4
  2.5 0.8 %copy-done.4 = s32[8192,1]{0,1:T(1,128)S(1)} copy-done((s32[8192,1]{0,1:T(1,128)S(1)}, s32[8192,1]{0,1:T(1,128)}, u32[]{:S(2)}) %copy-start.4) | copy-done | bytes 32792
  3.2 0.0 copy-start.5
  3.2 0.8 %copy-done.5 = s32[8192]{0:T(1024)S(1)} copy-done((s32[8192]{0:T(1024)S(1)}, s32[8192]{0:T(1024)}, u32[]{:S(2)}) %copy-start.5) | copy-done | bytes 32792
  4.0 0.0 copy-start.6
  4.0 0.8 %copy-done.6 = s32[8192,1]{0,1:T(1,128)S(1)} copy-done((s32[8192,1]{0,1:T(1,128)S(1)}, s32[8192,1]{0,1:T(1,128)}, u32[]{:S(2)}) %copy-start.6) | copy-done | bytes 32792
  4.7 0.0 copy-start.7
  4.7 0.8 %copy-done.7 = s32[8192]{0:T(1024)S(1)} copy-done((s32[8192]{0:T(1024)S(1)}, s32[8192]{0:T(1024)}, u32[]{:S(2)}) %copy-start.7) | copy-done | bytes 32792
  5.5 22.2 %relay_rows.1 = (f32[64,8,256]{2,1,0:T(8,128)S(1)}, s32[4,8,128]{2,1,0:T(8,128)S(1)}) custom-call(f32[3,8192]{1,0:T(4,128)S(1)} %copy-done.2, f32[1,8192]{1,0:T(1,128)S(1)} %bitcast.7, s32[1,8192]{1,0:T(1,128)S(1)} %bitcast.8, s32[1,8192]{1,0:T(1,128)S(1)} %bitcast.9, s32[1,8192]{1,0:T(1,128)S(1)} %bitcast.10, s32[1,8192]{1,0:T(1,128)S(1)} %bitcast.11), custom_call_target="tpu_custom_call" | custom-call | tf_op jit(solution)/shard_map/relay_rows/pallas_call | solution.py:228
  27.7 7.8 %scatter_rows.1 = f32[3,512,256]{2,1,0:T(8,128)S(1)} custom-call(s32[4,8,128]{2,1,0:T(8,128)S(1)} %get-tuple-element.4.slabs_of.slab_of, f32[64,8,256]{2,1,0:T(8,128)S(1)} %get-tuple-element.5.tiles), custom_call_target="tpu_custom_call" | custom-call | tf_op jit(solution)/shard_map/scatter_rows/pallas_call | solution.py:283
  35.5 0.0 copy-done
  35.5 0.0 copy-done.1
  35.5 32.2 %solve_rows.1 = (f32[3,16,32,256]{3,2,1,0:T(8,128)S(1)}, f32[3,64]{1,0:T(4,128)S(1)}) custom-call(s32[4,8,128]{2,1,0:T(8,128)S(1)} %get-tuple-element.4.slabs_of.slab_of, f32[64,8,256]{2,1,0:T(8,128)S(1)} %get-tuple-element.5.tiles, f32[3,16,32,256]{3,2,1,0:T(8,128)S(1)} %bitcast.6, f32[16,32,256]{2,1,0:T(8,128)S(1)} %copy-done.1, ...), custom_call_target="tpu_custom_call" | custom-call | tf_op jit(solution)/shard_map/solve_rows/pallas_call | solution.py:527
  67.7 1.1 %copy.13 = f32[3,16,32,256]{3,2,1,0:T(8,128)} copy(f32[3,16,32,256]{3,2,1,0:T(8,128)S(1)} %get-tuple-element.8) | data formatting | bytes 3145728
  68.9 0.6 copy.14
Async XLA Ops:
  0.6 34.8 %copy-start = (f32[3,16,32,256]{3,2,1,0:T(8,128)S(1)}, f32[3,16,32,256]{3,2,1,0:T(8,128)}, u32[]{:S(2)}) copy-start(f32[3,16,32,256]{3,2,1,0:T(8,128)} %anchor.1) | copy-start | bytes 4718596
  0.6 34.8 %copy-start.1 = (f32[16,32,256]{2,1,0:T(8,128)S(1)}, f32[16,32,256]{2,1,0:T(8,128)}, u32[]{:S(2)}) copy-start(f32[16,32,256]{2,1,0:T(8,128)} %stiff.1) | copy-start | bytes 1572868
  0.7 1.1 %copy-start.2 = (f32[3,8192]{1,0:T(4,128)S(1)}, f32[3,8192]{1,0:T(4,128)}, u32[]{:S(2)}) copy-start(f32[3,8192]{1,0:T(4,128)} %sens.1) | copy-start | bytes 294916
  1.7 0.8 %copy-start.3 = (f32[8192]{0:T(1024)S(1)}, f32[8192]{0:T(1024)}, u32[]{:S(2)}) copy-start(f32[8192]{0:T(1024)} %param.10) | copy-start | bytes 98308
  2.5 0.8 %copy-start.4 = (s32[8192,1]{0,1:T(1,128)S(1)}, s32[8192,1]{0,1:T(1,128)}, u32[]{:S(2)}) copy-start(s32[8192,1]{0,1:T(1,128)} %param.11) | copy-start | bytes 98308
  3.2 0.8 %copy-start.5 = (s32[8192]{0:T(1024)S(1)}, s32[8192]{0:T(1024)}, u32[]{:S(2)}) copy-start(s32[8192]{0:T(1024)} %param.12) | copy-start | bytes 98308
  4.0 0.8 %copy-start.6 = (s32[8192,1]{0,1:T(1,128)S(1)}, s32[8192,1]{0,1:T(1,128)}, u32[]{:S(2)}) copy-start(s32[8192,1]{0,1:T(1,128)} %param.13) | copy-start | bytes 98308
  4.7 0.8 %copy-start.7 = (s32[8192]{0:T(1024)S(1)}, s32[8192]{0:T(1024)}, u32[]{:S(2)}) copy-start(s32[8192]{0:T(1024)} %param.14) | copy-start | bytes 98308

commit v5 on v4

--- a/solution.py
+++ b/solution.py
@@ -9,7 +9,8 @@
 
 BOX_DEV = 64
 SWEEPS = 4
-SENT = 6
+SENT = 4
+FIELDS = 6
 NT = (((1,), (1,)), ((), ()))
 F32 = jnp.float32
 BF16 = jnp.bfloat16
@@ -83,7 +84,7 @@
     return jnp.sum(jnp.where(mask, value, 0.0), axis=0, keepdims=True)
 
 
-def relay_kernel(cut, slabs, parts, sens, weight, device, cell, owner, slot, tiles, slab_of, send, recv, place, spread, send_sem, recv_sem):
+def relay_kernel(cut, slabs, parts, sens, weight, device, cell, owner, slot, tiles, slab_of, spots, send, recv, place, spread, send_sem, recv_sem):
     count, fields, capacity = send.shape
     rows = sens.shape[1]
     _, _, width = tiles.shape
@@ -139,7 +140,7 @@
                     cell[:, span].astype(F32),
                     weight[:, span],
                     (owner[:, span] * BOX_DEV + slot[:, span]).astype(F32),
-                    jnp.zeros((fields - SENT, length), F32),
+                    jnp.zeros((fields - FIELDS, length), F32),
                 ],
                 axis=0,
             )
@@ -164,7 +165,7 @@
     senders = count // groups
     for group in reversed(range(groups)):
         lax.fori_loop(max(1, group * senders), (group + 1) * senders, arrive, 0)
-        sort_group(cut, slabs, [recv.at[group * senders + i] for i in range(senders)], tiles, group * per_group, per_group, slab_of, group)
+        sort_group(cut, slabs, [recv.at[group * senders + i] for i in range(senders)], tiles, group * per_group, per_group, slab_of, spots, group)
 
     def sent(step, carry):
         copy(step).wait_send()
@@ -173,17 +174,40 @@
     lax.fori_loop(1, count, sent, 0)
 
 
-def sort_group(cut, slabs, arrived, tiles, first, per_group, slab_of, group):
-    senders = len(arrived)
+def joined(arrived, low, high):
     fields, capacity = arrived[0].shape
+    join = max(1, min(len(arrived), 512 // capacity))
+    row = lax.broadcasted_iota(jnp.int32, (fields, join * capacity), 0)
+    return [
+        jnp.where(
+            (row >= low) & (row < high),
+            jnp.concatenate([arrived[q + i][...] for i in range(join)], axis=1),
+            0.0,
+        )
+        for q in range(0, len(arrived), join)
+    ]
+
+
+def ordered(blocks, spots, per_group, width):
+    fields = blocks[0].shape[0]
+    sums = jnp.zeros((per_group * 2 * fields, width), F32)
+    for block, spot in zip(blocks, spots):
+        tile, lane = split(spot, width)
+        terms = jnp.concatenate(two_terms(block), axis=0).astype(BF16)
+        tile = jnp.broadcast_to(tile, terms.shape).astype(jnp.int16)
+        spread = jnp.concatenate([kept(tile == t, terms) for t in range(per_group)], axis=0)
+        sums = sums + dot_nt(spread, wide_one_hot(width, lane))
+    made = []
+    for t in range(per_group):
+        at = t * 2 * fields
+        made.append(sums[at : at + fields] + sums[at + fields : at + 2 * fields])
+    return made
+
+
+def sort_group(cut, slabs, arrived, tiles, first, per_group, slab_of, spots, group):
     width = tiles.shape[2]
-    join = max(1, min(senders, 512 // capacity))
-    count = senders // join
-    real = lax.broadcasted_iota(jnp.int32, (fields, join * capacity), 0) < SENT
-    blocks = [
-        jnp.where(real, jnp.concatenate([arrived[q * join + i][...] for i in range(join)], axis=1), 0.0)
-        for q in range(count)
-    ]
+    blocks = joined(arrived, 0, SENT)
+    count = len(blocks)
     chosen = [matches(slabs, split(block[3:4].astype(jnp.int32), cut)[0]) for block in blocks]
     before, number = ordinals(chosen)
     total = running(number)
@@ -203,20 +227,18 @@
     slab = jnp.where(step[:1] < steps, slab, slabs)
     inside = (row > 0) & (start < (step + 1.0) * width)
     final = step[:1] + jnp.sum(jnp.where(inside, 1.0, 0.0), axis=0, keepdims=True)
-    table = jnp.concatenate([slab, final, jnp.zeros((6, 128), F32)], axis=0)
+    leave = jnp.sum(jnp.where(row == step + 1.0, entry, 0.0), axis=0, keepdims=True)
+    leave = jnp.where(step[:1] == slabs - 1, steps, leave) - 1.0
+    table = jnp.concatenate([slab, final, leave, jnp.zeros((5, 128), F32)], axis=0)
     slab_of[group] = table.astype(jnp.int32)
 
-    sums = jnp.zeros((per_group * 2 * fields, width), F32)
+    found = [
+        picked(chosen[q], before[q] + (total[q] + start)[:, :1]).astype(jnp.int32) for q in range(count)
+    ]
     for q in range(count):
-        where = picked(chosen[q], before[q] + (total[q] + start)[:, :1]).astype(jnp.int32)
-        tile, lane = split(where, width)
-        terms = jnp.concatenate(two_terms(blocks[q]), axis=0).astype(BF16)
-        tile = jnp.broadcast_to(tile, terms.shape).astype(jnp.int16)
-        spread = jnp.concatenate([kept(tile == t, terms) for t in range(per_group)], axis=0)
-        sums = sums + dot_nt(spread, wide_one_hot(width, lane))
-    for t in range(per_group):
-        at = t * 2 * fields
-        tiles[first + t] = sums[at : at + fields] + sums[at + fields : at + 2 * fields]
+        spots[group * count + q : group * count + q + 1] = found[q]
+    for t, tile in enumerate(ordered(blocks, found, per_group, width)):
+        tiles[first + t] = tile
 
 
 def relay_rows(devices, capacity, slabs, cut, sens, weight, device, cell, owner, slot):
@@ -225,22 +247,24 @@
     width = min(256, size)
     groups = rows // size
     parts = 2
+    length = max(1, min(size // capacity, 512 // capacity)) * capacity
     return pl.pallas_call(
         functools.partial(relay_kernel, cut, slabs, parts),
         out_shape=[
             jax.ShapeDtypeStruct((rows // width, 8, width), F32),
             jax.ShapeDtypeStruct((groups, 8, 128), jnp.int32),
+            jax.ShapeDtypeStruct((rows // length, length), jnp.int32),
+            jax.ShapeDtypeStruct((devices, 8, capacity), F32),
         ],
         in_specs=[pl.BlockSpec(memory_space=pltpu.VMEM)] * 6,
-        out_specs=[pl.BlockSpec(memory_space=pltpu.VMEM)] * 2,
+        out_specs=[pl.BlockSpec(memory_space=pltpu.VMEM)] * 4,
         scratch_shapes=[
-            pltpu.VMEM((devices, 8, capacity), F32),
             pltpu.VMEM((devices, 8, capacity), F32),
             pltpu.VMEM((capacity, sens.shape[1]), BF16),
             pltpu.VMEM((devices // parts * 16, sens.shape[1]), BF16),
         ]
         + [pltpu.SemaphoreType.DMA((devices,))] * 2,
-        compiler_params=pltpu.CompilerParams(collective_id=1, has_side_effects=True, vmem_limit_bytes=48 << 20),
+        compiler_params=pltpu.CompilerParams(collective_id=1, has_side_effects=True, vmem_limit_bytes=60 << 20),
         name="relay_rows",
     )(sens, weight, device, cell, owner, slot)
 
@@ -249,49 +273,13 @@
     return split(tile[3:4].astype(jnp.int32), size_z)
 
 
-def scatter_kernel(size_y, slabs_of, tiles, load):
-    parts, size_xy, size_z = load.shape
-    groups = slabs_of.shape[0]
-    per_group = tiles.shape[0] // groups
-    slabs = size_xy // size_y
+def solve_kernel(slab_of, tiles, spots, parcels, stiff_in, anchor_in, coupling_in, adjoint, box, stiff, anchor, coupling, load, stage, late, marks, weighted, inverse, near, edge, halo, terms, found, flat, landed, fetch, late_send, late_recv, x_send, x_recv, y_send, y_recv, box_send, box_recv):
+    parts, size_x, size_y, size_z = load.shape
+    count, _, width = tiles.shape
+    groups = slab_of.shape[0]
+    per_group = count // groups
+    steps = per_group + size_x
     half = parts * size_y
-    load[...] = jnp.zeros_like(load)
-
-    def body(step, carry):
-        made = []
-        for group in range(groups):
-            slab = slabs_of[group, 0, step]
-            tile = tiles[group * per_group + jnp.minimum(step - slab, per_group - 1)]
-            xy, z = located(tile, size_z)
-            at_z = wide_one_hot(size_z, z)
-            pairs = [two_terms(tile[k : k + 1]) for k in range(parts)]
-            values = [hi for hi, lo in pairs] + [lo for hi, lo in pairs]
-            at_y = matches(size_y, xy - slab * size_y)
-            terms = jnp.concatenate([scaled(at_y, value) for value in values], axis=0)
-            product = dot_nt(terms, at_z)
-            made.append((slab, product[:half] + product[half:]))
-        for slab, product in made:
-            span = pl.ds(pl.multiple_of(jnp.minimum(slab, slabs - 1) * size_y, size_y), size_y)
-            for k in range(parts):
-                load[k, span] = load[k, span] + product[k * size_y : (k + 1) * size_y]
-        return carry
-
-    lax.fori_loop(0, per_group + slabs, body, 0, unroll=4)
-
-
-def scatter_rows(tiles, ends, size_x, size_y, size_z):
-    return pl.pallas_call(
-        functools.partial(scatter_kernel, size_y),
-        out_shape=jax.ShapeDtypeStruct((3, size_x * size_y, size_z), F32),
-        in_specs=[pl.BlockSpec(memory_space=pltpu.SMEM), pl.BlockSpec(memory_space=pltpu.VMEM)],
-        out_specs=pl.BlockSpec(memory_space=pltpu.VMEM),
-        compiler_params=pltpu.CompilerParams(vmem_limit_bytes=32 << 20),
-        name="scatter_rows",
-    )(ends, tiles)
-
-
-def solve_kernel(slab_of, tiles, load, stiff, anchor, coupling, adjoint, box, weighted, inverse, near, edge, halo, terms, found, flat, landed, x_send, x_recv, y_send, y_recv, box_send, box_recv):
-    parts, size_x, size_y, size_z = load.shape
     exchanges = weighted.shape[0]
     gx, gy = lax.axis_index("gx"), lax.axis_index("gy")
     count_x, count_y = lax.axis_size("gx"), lax.axis_size("gy")
@@ -311,6 +299,12 @@
         return carry
 
     lax.fori_loop(1, devices, greet, 0)
+    fetches = [
+        pltpu.make_async_copy(source, target, fetch.at[i])
+        for i, (source, target) in enumerate(((stiff_in, stiff), (anchor_in, anchor), (coupling_in, coupling)))
+    ]
+    for copy in fetches:
+        copy.start()
 
     for side, (axis, place, move, present) in enumerate(sides):
 
@@ -362,14 +356,72 @@
 
     rims = (0, size_y - 1)
 
+    def deposit(step, carry):
+        made = []
+        for group in range(groups):
+            slab = slab_of[group, 0, step]
+            tile = tiles[group * per_group + jnp.minimum(step - slab, per_group - 1)]
+            xy, z = located(tile, size_z)
+            pairs = [two_terms(tile[k : k + 1]) for k in range(parts)]
+            values = [hi for hi, lo in pairs] + [lo for hi, lo in pairs]
+            at_y = matches(size_y, xy - slab * size_y)
+            spread = jnp.concatenate([scaled(at_y, value) for value in values], axis=0)
+            product = dot_nt(spread, wide_one_hot(size_z, z))
+            at = group * steps + step
+            earlier = stage[jnp.maximum(at - 1, 0)]
+            stage[at] = product[:half] + product[half:] + jnp.where(slab == carry[group], earlier, 0.0)
+            made.append(slab)
+        return tuple(made)
+
+    late_rows = pl.ds(SENT, FIELDS - SENT)
+
+    def follow(step):
+        return pltpu.make_async_remote_copy(
+            src_ref=parcels.at[step, late_rows],
+            dst_ref=late.at[step, late_rows],
+            send_sem=late_send.at[step],
+            recv_sem=late_recv.at[step],
+            device_id=peer(step),
+            device_id_type=MESH,
+        )
+
+    def send_late(step, carry):
+        follow(step).start()
+        return carry
+
+    def take_late(step, carry):
+        follow(step).wait_recv()
+        return carry
+
+    def sort_late(group):
+        senders = devices // groups
+        blocks = joined([late.at[group * senders + i] for i in range(senders)], SENT, FIELDS)
+        lines = [spots[q : q + 1] for q in range(group * len(blocks), (group + 1) * len(blocks))]
+        for t, tile in enumerate(ordered(blocks, lines, per_group, width)):
+            marks[group * per_group + t] = tile
+
+    stage[0] = jnp.zeros(stage.shape[1:], F32)
+    slabs = lax.fori_loop(0, steps // 2, deposit, tuple(jnp.int32(-1) for _ in range(groups)), unroll=4)
+    pl.semaphore_wait(barrier, devices - 1)
+    lax.fori_loop(1, devices, send_late, 0)
+    late[0] = parcels[0]
+    lax.fori_loop(steps // 2, steps, deposit, slabs, unroll=4)
+    for copy in fetches:
+        copy.wait()
+
     def first(x, carry):
         stiffness = stiff[x]
+        sums = stage[slab_of[0, 2, x]]
+        for group in range(1, groups):
+            sums = sums + stage[group * steps + slab_of[group, 2, x]]
         for side, rim in enumerate(rims):
             near[2, side, 0, pl.ds(x, 1), :] = stiffness[rim : rim + 1]
         for k in range(parts):
             inverted = 1.0 / (6.0 * stiffness + anchor[k, x] + coupling[4 * k, x])
             inverse[k, x] = inverted
-            value = load[k, x] * inverted
+            there = sums[k * size_y : (k + 1) * size_y]
+            load[k, x] = there
+            value = there * inverted
             adjoint[k, x] = value
             product = stiffness * value
             weighted[0, k, x + 1] = product
@@ -379,11 +431,13 @@
         return carry
 
     lax.fori_loop(0, size_x, first, 0)
-    pl.semaphore_wait(barrier, devices - 1)
     begin(0)
+    lax.fori_loop(1, devices, take_late, 0)
 
     for index in range(exchanges):
         last = index + 1 == exchanges
+        for group in range(groups * index // exchanges, groups * (index + 1) // exchanges):
+            sort_late(group)
 
         def update(x, carry):
             fields = [adjoint[k, x] for k in range(parts)]
@@ -423,12 +477,6 @@
         if not last:
             begin(index + 1)
 
-    count, _, width = tiles.shape
-    groups = slab_of.shape[0]
-    per_group = count // groups
-    steps = per_group + size_x
-    half = parts * size_y
-
     def cut(x, carry):
         for k in range(parts):
             hi, lo = two_terms(adjoint[k, x])
@@ -465,7 +513,7 @@
         numbers = range(begin_at, begin_at + join)
 
         def line(field):
-            return jnp.concatenate([tiles[t, field : field + 1] for t in numbers], axis=1)
+            return jnp.concatenate([marks[t, field : field + 1] for t in numbers], axis=1)
 
         owner, slot = split(line(5).astype(jnp.int32), BOX_DEV)
         rows = jnp.concatenate(
@@ -510,6 +558,12 @@
         return carry
 
     lax.fori_loop(1, devices, sent, 0)
+
+    def left(step, carry):
+        follow(step).wait_send()
+        return carry
+
+    lax.fori_loop(1, devices, left, 0)
     for index in range(exchanges):
         for present, copy in transfers(index, True):
 
@@ -518,20 +572,30 @@
                 copy.wait_send()
 
 
-def solve_rows(devices, tiles, slab_of, load, stiffness, anchor, coupling):
-    parts, size_x, size_y, size_z = load.shape
+def solve_rows(devices, tiles, slab_of, spots, parcels, stiffness, anchor, coupling):
+    size_x, size_y, size_z = stiffness.shape
+    parts = anchor.shape[0]
     exchanges = SWEEPS - 1
     count, fields, width = tiles.shape
     groups = slab_of.shape[0]
     steps = count // groups + size_x
     return pl.pallas_call(
         solve_kernel,
-        out_shape=[jax.ShapeDtypeStruct(load.shape, F32), jax.ShapeDtypeStruct((parts, BOX_DEV), F32)],
-        in_specs=[pl.BlockSpec(memory_space=pltpu.SMEM)] + [pl.BlockSpec(memory_space=pltpu.VMEM)] * 5,
+        out_shape=[jax.ShapeDtypeStruct(anchor.shape, F32), jax.ShapeDtypeStruct((parts, BOX_DEV), F32)],
+        in_specs=[pl.BlockSpec(memory_space=pltpu.SMEM)]
+        + [pl.BlockSpec(memory_space=pltpu.VMEM)] * 3
+        + [pl.BlockSpec(memory_space=pl.ANY)] * 3,
         out_specs=[pl.BlockSpec(memory_space=pltpu.VMEM)] * 2,
         scratch_shapes=[
+            pltpu.VMEM(stiffness.shape, F32),
+            pltpu.VMEM(anchor.shape, F32),
+            pltpu.VMEM(coupling.shape, F32),
+            pltpu.VMEM(anchor.shape, F32),
+            pltpu.VMEM((groups * steps, parts * size_y, size_z), F32),
+            pltpu.VMEM(parcels.shape, F32),
+            pltpu.VMEM(tiles.shape, F32),
             pltpu.VMEM((exchanges, parts, size_x + 2, size_y, size_z), F32),
-            pltpu.VMEM(load.shape, F32),
+            pltpu.VMEM(anchor.shape, F32),
             pltpu.VMEM((3, 2, parts, size_x, size_z), F32),
             pltpu.VMEM((exchanges, 2, parts, size_x, size_z), F32),
             pltpu.VMEM((exchanges, 2, parts, size_x, size_z), F32),
@@ -539,12 +603,14 @@
             pltpu.VMEM((groups * steps, fields, width), F32),
             pltpu.VMEM((parts, devices, 2 * BOX_DEV), F32),
             pltpu.VMEM((parts, devices, 2 * BOX_DEV), F32),
+            pltpu.SemaphoreType.DMA((3,)),
         ]
+        + [pltpu.SemaphoreType.DMA((devices,))] * 2
         + [pltpu.SemaphoreType.DMA((exchanges, 2))] * 4
         + [pltpu.SemaphoreType.DMA((devices,))] * 2,
-        compiler_params=pltpu.CompilerParams(collective_id=0, has_side_effects=True, vmem_limit_bytes=48 << 20),
+        compiler_params=pltpu.CompilerParams(collective_id=0, has_side_effects=True, vmem_limit_bytes=60 << 20),
         name="solve_rows",
-    )(slab_of, tiles, load, stiffness, anchor, coupling)
+    )(slab_of, tiles, spots, parcels, stiffness, anchor, coupling)
 
 
 def body(
@@ -568,7 +634,7 @@
     def row(values):
         return values.reshape(1, row_count)
 
-    tiles, ends = relay_rows(
+    tiles, slab_of, spots, parcels = relay_rows(
         devices,
         capacity,
         size_x,
@@ -580,9 +646,7 @@
         row(box_owner),
         row(box_slot),
     )
-    load = scatter_rows(tiles, ends, size_x, size_y, size_z)
-    load = load.reshape(3, size_x, size_y, size_z)
-    adjoint, box_gradient = solve_rows(devices, tiles, ends, load, stiffness, anchor, coupling)
+    adjoint, box_gradient = solve_rows(devices, tiles, slab_of, spots, parcels, stiffness, anchor, coupling)
     return (adjoint, box_gradient)
 
 

time: 69.9 us -> 66.5 us (0.951)
  local copies, waits for them, and re-layouts: 6.56 us -> 3.31 us
    unnamed x18 -> x4, local copies, waits for them, and re-layouts: 6.56 us -> 3.31 us
    pallas_call x2 -> x1, Pallas kernels: 40 us -> 41.2 us  [solve_rows(): pl.pallas_call(solve_kernel, out_shape=[jax.ShapeDtypeStruct(anchor.shape...]
    pallas_call x1, Pallas kernels: 22.2 us -> 21.1 us  [relay_rows(): pl.pallas_call(functools.partial(relay_kernel, cut, slabs, parts), out_sh...]
where the time goes in v5:
time: 66.5 us; the launch traced here: 66.3 us
  Pallas kernels  62.3 us (94%)
  local copies, waits for them, and re-layouts  3.31 us (5%)
    pallas_call x1, Pallas kernels, solve_rows(): pl.pallas_call(solve_kernel, out_shape=[jax.ShapeDtypeStruct(anchor.shape...  41.2 us
    pallas_call x1, Pallas kernels, relay_rows(): pl.pallas_call(functools.partial(relay_kernel, cut, slabs, parts), out_sh...  21.1 us
    unnamed x4, local copies, waits for them, and re-layouts  3.31 us

profile of v5, /device:TPU:0, one launch (start us, length us, event | category | flops | bytes accessed | tf_op | source)
XLA Modules:
  0.0 66.3 jit_solution(12913756396508257182)
XLA Ops:
  0.6 21.1 %relay_rows.1 = (f32[64,8,256]{2,1,0:T(8,128)}, s32[4,8,128]{2,1,0:T(8,128)}, s32[32,512]{1,0:T(8,128)}, f32[32,8,512]{2,1,0:T(8,128)}) custom-call(f32[3,8192]{1,0:T(4,128)} %sens.1, f32[1,8192]{1,0:T(1,128)} %bitcast.5, s32[1,8192]{1,0:T(1,128)} %bitcast.6, s32[1,8192]{1,0:T(1,128)} %bitcast.7, s32[1,8192]{1,0:T(1,128)} %bitcast.8, s32[1,8192]{1,0:T(1,128)} %bitcast.9), custom_call_target="tpu_custom_call" | custom-call | tf_op jit(solution)/shard_map/relay_rows/pallas_call | solution.py:251
  21.7 41.2 %solve_rows.1 = (f32[3,16,32,256]{3,2,1,0:T(8,128)}, f32[3,64]{1,0:T(4,128)}) custom-call(s32[4,8,128]{2,1,0:T(8,128)} %get-tuple-element.6.slab_of, f32[64,8,256]{2,1,0:T(8,128)} %get-tuple-element.7.tiles, s32[32,512]{1,0:T(8,128)} %get-tuple-element.8.spots, f32[32,8,512]{2,1,0:T(8,128)} %get-tuple-element.9.parcels, f32[16,32,256]{2,1,0:T(8,128)} %stiff_in.1, ...), custom_call_target="tpu_custom_call" | custom-call | tf_op jit(solution)/shard_map/solve_rows/pallas_call | solution.py:582
  63.0 0.0 copy-start
  63.0 2.7 %copy.13 = f32[3,16,32,256]{3,2,1,0:T(8,128)} copy(f32[3,16,32,256]{3,2,1,0:T(8,128)} %get-tuple-element.12) | data formatting | bytes 3145728
  65.7 0.0 copy-done
  65.7 0.6 copy.14
Async XLA Ops:
  63.0 2.7 %copy-start = (f32[3,64]{1,0:T(4,128)S(1)}, f32[3,64]{1,0:T(4,128)}, u32[]{:S(2)}) copy-start(f32[3,64]{1,0:T(4,128)} %get-tuple-element.13) | copy-start | bytes 2308

commit v6 on v5

--- a/solution.py
+++ b/solution.py
@@ -54,6 +54,20 @@
 
 def kept(mask, values):
     return jnp.where(mask, values, jnp.array(0, BF16))
+
+
+def folded(a, b, size):
+    if size & (size - 1):
+        return (a + b) % size
+    total, bit = 0, 1
+    while bit < size:
+        total = total + bit * ((a // bit + b // bit) % 2)
+        bit = 2 * bit
+    return total
+
+
+def peer_of(gx, gy, size_x, size_y):
+    return lambda step: (folded(gx, step // size_y, size_x), (gy + step % size_y) % size_y)
 
 
 def running(numbers):
@@ -84,7 +98,9 @@
     return jnp.sum(jnp.where(mask, value, 0.0), axis=0, keepdims=True)
 
 
-def relay_kernel(cut, slabs, parts, sens, weight, device, cell, owner, slot, tiles, slab_of, spots, send, recv, place, spread, send_sem, recv_sem):
+def relay_kernel(cut, slabs, parts, *refs):
+    given, refs = refs[:6], refs[6:]
+    tiles, slab_of, spots, send, sens, weight, device, cell, owner, slot, recv, place, spread, fetch, send_sem, recv_sem = refs
     count, fields, capacity = send.shape
     rows = sens.shape[1]
     _, _, width = tiles.shape
@@ -92,12 +108,14 @@
     per_group = tiles.shape[0] // groups
     gx, gy = lax.axis_index("gx"), lax.axis_index("gy")
     size_x, size_y = lax.axis_size("gx"), lax.axis_size("gy")
-    me = gx * size_y + gy
+    peer = peer_of(gx, gy, size_x, size_y)
     barrier = pltpu.get_barrier_semaphore()
-
-    def peer(step):
-        there = (me + step) % count
-        return (there // size_y, there % size_y)
+    fetches = [
+        pltpu.make_async_copy(source, target, fetch.at[i])
+        for i, (source, target) in enumerate(zip(given, (sens, weight, device, cell, owner, slot)))
+    ]
+    for copy in fetches:
+        copy.start()
 
     def greet(step, carry):
         pl.semaphore_signal(barrier, inc=1, device_id=peer(step), device_id_type=MESH)
@@ -108,8 +126,17 @@
     length = min(512, rows)
     chunks = rows // length
     spans = [slice(q * length, (q + 1) * length) for q in range(chunks)]
-    target = device[...] - me
-    target = jnp.where(target < 0, target + count, target)
+    for copy in fetches:
+        copy.wait()
+    to_x, to_y = split(device[...], size_y)
+    to_y = to_y - gy
+    to_y = jnp.where(to_y < 0, to_y + size_y, to_y)
+    if size_x & (size_x - 1):
+        to_x = to_x - gx
+        to_x = jnp.where(to_x < 0, to_x + size_x, to_x)
+    else:
+        to_x = to_x ^ gx
+    target = to_x * size_y + to_y
     chosen = [matches(count, target[:, span]) for span in spans]
     before, number = ordinals(chosen)
     total = running(number)
@@ -163,7 +190,7 @@
         return carry
 
     senders = count // groups
-    for group in reversed(range(groups)):
+    for group in range(groups):
         lax.fori_loop(max(1, group * senders), (group + 1) * senders, arrive, 0)
         sort_group(cut, slabs, [recv.at[group * senders + i] for i in range(senders)], tiles, group * per_group, per_group, slab_of, spots, group)
 
@@ -251,17 +278,19 @@
     return pl.pallas_call(
         functools.partial(relay_kernel, cut, slabs, parts),
         out_shape=[
-            jax.ShapeDtypeStruct((rows // width, 8, width), F32),
+            pltpu.VMEM((rows // width, 8, width), F32),
             jax.ShapeDtypeStruct((groups, 8, 128), jnp.int32),
-            jax.ShapeDtypeStruct((rows // length, length), jnp.int32),
-            jax.ShapeDtypeStruct((devices, 8, capacity), F32),
+            pltpu.VMEM((rows // length, length), jnp.int32),
+            pltpu.VMEM((devices, 8, capacity), F32),
         ],
-        in_specs=[pl.BlockSpec(memory_space=pltpu.VMEM)] * 6,
+        in_specs=[pl.BlockSpec(memory_space=pltpu.HBM)] * 6,
         out_specs=[pl.BlockSpec(memory_space=pltpu.VMEM)] * 4,
-        scratch_shapes=[
+        scratch_shapes=[pltpu.VMEM(given.shape, given.dtype) for given in (sens, weight, device, cell, owner, slot)]
+        + [
             pltpu.VMEM((devices, 8, capacity), F32),
             pltpu.VMEM((capacity, sens.shape[1]), BF16),
             pltpu.VMEM((devices // parts * 16, sens.shape[1]), BF16),
+            pltpu.SemaphoreType.DMA((6,)),
         ]
         + [pltpu.SemaphoreType.DMA((devices,))] * 2,
         compiler_params=pltpu.CompilerParams(collective_id=1, has_side_effects=True, vmem_limit_bytes=60 << 20),
@@ -284,15 +313,11 @@
     gx, gy = lax.axis_index("gx"), lax.axis_index("gy")
     count_x, count_y = lax.axis_size("gx"), lax.axis_size("gy")
     devices = count_x * count_y
-    me = gx * count_y + gy
+    peer = peer_of(gx, gy, count_x, count_y)
     sides = (("gx", gx, -1, gx > 0), ("gx", gx, 1, gx < count_x - 1), ("gy", gy, -1, gy > 0), ("gy", gy, 1, gy < count_y - 1))
     y_at = lax.broadcasted_iota(jnp.int32, (size_y, size_z), 0)
     z_at = lax.broadcasted_iota(jnp.int32, (size_y, size_z), 1)
     barrier = pltpu.get_barrier_semaphore()
-
-    def peer(step):
-        there = (me + step) % devices
-        return (there // count_y, there % count_y)
 
     def greet(step, carry):
         pl.semaphore_signal(barrier, inc=1, device_id=peer(step), device_id_type=MESH)
@@ -386,7 +411,7 @@
         )
 
     def send_late(step, carry):
-        follow(step).start()
+        follow(devices - step).start()
         return carry
 
     def take_late(step, carry):
@@ -401,11 +426,11 @@
             marks[group * per_group + t] = tile
 
     stage[0] = jnp.zeros(stage.shape[1:], F32)
-    slabs = lax.fori_loop(0, steps // 2, deposit, tuple(jnp.int32(-1) for _ in range(groups)), unroll=4)
+    slabs = lax.fori_loop(0, steps // 2, deposit, tuple(jnp.int32(-1) for _ in range(groups)), unroll=8)
     pl.semaphore_wait(barrier, devices - 1)
     lax.fori_loop(1, devices, send_late, 0)
     late[0] = parcels[0]
-    lax.fori_loop(steps // 2, steps, deposit, slabs, unroll=4)
+    lax.fori_loop(steps // 2, steps, deposit, slabs, unroll=8)
     for copy in fetches:
         copy.wait()
 
@@ -529,21 +554,22 @@
         flat[k] = jnp.concatenate([part, jnp.zeros_like(part)], axis=1)
 
     def parcel(step):
+        there = peer(step)
         return pltpu.make_async_remote_copy(
-            src_ref=flat.at[:, pl.ds((me + step) % devices, 1)],
+            src_ref=flat.at[:, pl.ds(there[0] * count_y + there[1], 1)],
             dst_ref=landed.at[:, pl.ds(step, 1)],
             send_sem=box_send.at[step],
             recv_sem=box_recv.at[step],
-            device_id=peer(step),
+            device_id=there,
             device_id_type=MESH,
         )
 
     def post(step, carry):
-        parcel(step).start()
+        parcel(devices - step).start()
         return carry
 
     lax.fori_loop(1, devices, post, 0)
-    landed[:, 0:1] = flat[:, pl.ds(me, 1)]
+    landed[:, 0:1] = flat[:, pl.ds(gx * count_y + gy, 1)]
 
     def collect(step, carry):
         parcel(step).wait_recv()
@@ -579,12 +605,13 @@
     count, fields, width = tiles.shape
     groups = slab_of.shape[0]
     steps = count // groups + size_x
+    kept_near = [pltpu.with_memory_space_constraint(value, pltpu.VMEM) for value in (tiles, spots, parcels)]
     return pl.pallas_call(
         solve_kernel,
-        out_shape=[jax.ShapeDtypeStruct(anchor.shape, F32), jax.ShapeDtypeStruct((parts, BOX_DEV), F32)],
+        out_shape=[pltpu.VMEM(anchor.shape, F32), pltpu.VMEM((parts, BOX_DEV), F32)],
         in_specs=[pl.BlockSpec(memory_space=pltpu.SMEM)]
         + [pl.BlockSpec(memory_space=pltpu.VMEM)] * 3
-        + [pl.BlockSpec(memory_space=pl.ANY)] * 3,
+        + [pl.BlockSpec(memory_space=pltpu.HBM)] * 3,
         out_specs=[pl.BlockSpec(memory_space=pltpu.VMEM)] * 2,
         scratch_shapes=[
             pltpu.VMEM(stiffness.shape, F32),
@@ -608,9 +635,9 @@
         + [pltpu.SemaphoreType.DMA((devices,))] * 2
         + [pltpu.SemaphoreType.DMA((exchanges, 2))] * 4
         + [pltpu.SemaphoreType.DMA((devices,))] * 2,
-        compiler_params=pltpu.CompilerParams(collective_id=0, has_side_effects=True, vmem_limit_bytes=60 << 20),
+        compiler_params=pltpu.CompilerParams(collective_id=0, has_side_effects=True, vmem_limit_bytes=56 << 20),
         name="solve_rows",
-    )(slab_of, tiles, spots, parcels, stiffness, anchor, coupling)
+    )(slab_of, *kept_near, stiffness, anchor, coupling)
 
 
 def body(

time: 66.5 us -> 62 us (0.932)
  Pallas kernels: 62.3 us -> 59.4 us
  local copies, waits for them, and re-layouts: 3.31 us -> 1.72 us
    pallas_call x1, Pallas kernels: 41.2 us -> 37.2 us  [solve_rows(): pl.pallas_call(solve_kernel, out_shape=[pltpu.VMEM(anchor.shape, F32), pl...]
    unnamed x4 -> x2, local copies, waits for them, and re-layouts: 3.31 us -> 1.72 us
    pallas_call x1, Pallas kernels: 21.1 us -> 22.3 us  [relay_rows(): pl.pallas_call(functools.partial(relay_kernel, cut, slabs, parts), out_sh...]
where the time goes in v6:
time: 62 us; the launch traced here: 61.8 us
  Pallas kernels  59.4 us (96%)
  local copies, waits for them, and re-layouts  1.72 us (3%)
  between operations  0.65 us (1%)
    pallas_call x1, Pallas kernels, solve_rows(): pl.pallas_call(solve_kernel, out_shape=[pltpu.VMEM(anchor.shape, F32), pl...  37.2 us
    pallas_call x1, Pallas kernels, relay_rows(): pl.pallas_call(functools.partial(relay_kernel, cut, slabs, parts), out_sh...  22.3 us
    unnamed x2, local copies, waits for them, and re-layouts  1.72 us

profile of v6, /device:TPU:0, one launch (start us, length us, event | category | flops | bytes accessed | tf_op | source)
XLA Modules:
  0.0 61.8 jit_solution(3480250400135270651)
XLA Ops:
  0.6 22.3 %relay_rows.1 = (f32[64,8,256]{2,1,0:T(8,128)S(1)}, s32[4,8,128]{2,1,0:T(8,128)}, s32[32,512]{1,0:T(8,128)S(1)}, f32[32,8,512]{2,1,0:T(8,128)S(1)}) custom-call(f32[3,8192]{1,0:T(4,128)} %refs_0_.1, f32[1,8192]{1,0:T(1,128)} %bitcast.5, s32[1,8192]{1,0:T(1,128)} %bitcast.6, s32[1,8192]{1,0:T(1,128)} %bitcast.7, s32[1,8192]{1,0:T(1,128)} %bitcast.8, ...), custom_call_target="tpu_custom_call" | custom-call | tf_op jit(solution)/shard_map/relay_rows/pallas_call | solution.py:278
  22.9 37.2 %solve_rows.1 = (f32[3,16,32,256]{3,2,1,0:T(8,128)S(1)}, f32[3,64]{1,0:T(4,128)S(1)}) custom-call(s32[4,8,128]{2,1,0:T(8,128)} %get-tuple-element.6.slab_of, f32[64,8,256]{2,1,0:T(8,128)S(1)} %get-tuple-element.7.tiles, s32[32,512]{1,0:T(8,128)S(1)} %get-tuple-element.8.spots, f32[32,8,512]{2,1,0:T(8,128)S(1)} %get-tuple-element.9.parcels, ...), custom_call_target="tpu_custom_call" | custom-call | tf_op jit(solution)/shard_map/solve_rows/pallas_call | solution.py:609
  60.1 1.1 %copy.13 = f32[3,16,32,256]{3,2,1,0:T(8,128)} copy(f32[3,16,32,256]{3,2,1,0:T(8,128)S(1)} %get-tuple-element.10) | data formatting | bytes 3145728
  61.2 0.6 copy.14

commit v7 on v6

--- a/solution.py
+++ b/solution.py
@@ -54,6 +54,24 @@
 
 def kept(mask, values):
     return jnp.where(mask, values, jnp.array(0, BF16))
+
+
+def fan(values, index, count):
+    size, length = values.shape
+    many = min(count, max(1, 16 // size))
+    terms = jnp.concatenate([values] * many, axis=0).astype(BF16)
+    part = lax.broadcasted_iota(jnp.int32, terms.shape, 0) // size
+    index = (jnp.broadcast_to(index, terms.shape) - part).astype(jnp.int16)
+    return jnp.concatenate([kept(index == t, terms) for t in range(0, count, many)], axis=0)
+
+
+def two_rows(rows):
+    return jnp.concatenate(two_terms(jnp.concatenate(rows, axis=0)), axis=0)
+
+
+def halves(values):
+    size = values.shape[0] // 2
+    return values[:size] + values[size:]
 
 
 def folded(a, b, size):
@@ -98,7 +116,7 @@
     return jnp.sum(jnp.where(mask, value, 0.0), axis=0, keepdims=True)
 
 
-def relay_kernel(cut, slabs, parts, *refs):
+def relay_kernel(cut, slabs, *refs):
     given, refs = refs[:6], refs[6:]
     tiles, slab_of, spots, send, sens, weight, device, cell, owner, slot, recv, place, spread, fetch, send_sem, recv_sem = refs
     count, fields, capacity = send.shape
@@ -158,31 +176,18 @@
         copy(step).start()
         return carry
 
-    share = count // parts
-    for part in reversed(range(parts)):
-        for q, span in enumerate(spans):
-            payload = jnp.concatenate(
-                [
-                    sens[:, span],
-                    cell[:, span].astype(F32),
-                    weight[:, span],
-                    (owner[:, span] * BOX_DEV + slot[:, span]).astype(F32),
-                    jnp.zeros((fields - FIELDS, length), F32),
-                ],
-                axis=0,
-            )
-            terms = jnp.concatenate(two_terms(payload), axis=0).astype(BF16)
-            to = jnp.broadcast_to(target[:, span] - part * share, terms.shape).astype(jnp.int16)
-            for t in range(share):
-                spread[t * 2 * fields : (t + 1) * 2 * fields, span] = kept(to == t, terms)
-        product = dot_nt(spread[...], place[...])
-        for t in range(share):
-            at = t * 2 * fields
-            send[part * share + t] = product[at : at + fields] + product[at + fields : at + 2 * fields]
-        if part == parts - 1:
-            pl.semaphore_wait(barrier, count - 1)
-        lax.fori_loop(max(1, part * share), (part + 1) * share, start, 0)
-
+    def packed(rows, low):
+        size = 2 * len(rows)
+        for span in spans:
+            spread[: count * size, span] = fan(two_rows([read(span) for read in rows]), target[:, span], count)
+        product = dot_nt(spread[: count * size], place[...])
+        for t in range(count):
+            send[t, low : low + len(rows)] = halves(product[t * size : (t + 1) * size])
+
+    packed([lambda span, k=k: sens[k : k + 1, span] for k in range(3)] + [lambda span: cell[:, span].astype(F32)], 0)
+    pl.semaphore_wait(barrier, count - 1)
+    lax.fori_loop(1, count, start, 0)
+    packed([lambda span: weight[:, span], lambda span: (owner[:, span] * BOX_DEV + slot[:, span]).astype(F32)], SENT)
     recv[0] = send[0]
 
     def arrive(step, carry):
@@ -202,33 +207,21 @@
 
 
 def joined(arrived, low, high):
-    fields, capacity = arrived[0].shape
-    join = max(1, min(len(arrived), 512 // capacity))
-    row = lax.broadcasted_iota(jnp.int32, (fields, join * capacity), 0)
+    join = max(1, min(len(arrived), 512 // arrived[0].shape[1]))
     return [
-        jnp.where(
-            (row >= low) & (row < high),
-            jnp.concatenate([arrived[q + i][...] for i in range(join)], axis=1),
-            0.0,
-        )
+        jnp.concatenate([arrived[q + i][low:high] for i in range(join)], axis=1)
         for q in range(0, len(arrived), join)
     ]
 
 
 def ordered(blocks, spots, per_group, width):
-    fields = blocks[0].shape[0]
-    sums = jnp.zeros((per_group * 2 * fields, width), F32)
+    size = 2 * blocks[0].shape[0]
+    sums = jnp.zeros((per_group * size, width), F32)
     for block, spot in zip(blocks, spots):
         tile, lane = split(spot, width)
-        terms = jnp.concatenate(two_terms(block), axis=0).astype(BF16)
-        tile = jnp.broadcast_to(tile, terms.shape).astype(jnp.int16)
-        spread = jnp.concatenate([kept(tile == t, terms) for t in range(per_group)], axis=0)
+        spread = fan(jnp.concatenate(two_terms(block), axis=0), tile, per_group)
         sums = sums + dot_nt(spread, wide_one_hot(width, lane))
-    made = []
-    for t in range(per_group):
-        at = t * 2 * fields
-        made.append(sums[at : at + fields] + sums[at + fields : at + 2 * fields])
-    return made
+    return [halves(sums[t * size : (t + 1) * size]) for t in range(per_group)]
 
 
 def sort_group(cut, slabs, arrived, tiles, first, per_group, slab_of, spots, group):
@@ -265,7 +258,7 @@
     for q in range(count):
         spots[group * count + q : group * count + q + 1] = found[q]
     for t, tile in enumerate(ordered(blocks, found, per_group, width)):
-        tiles[first + t] = tile
+        tiles[first + t, :SENT] = tile
 
 
 def relay_rows(devices, capacity, slabs, cut, sens, weight, device, cell, owner, slot):
@@ -273,10 +266,9 @@
     size = min(4096, rows)
     width = min(256, size)
     groups = rows // size
-    parts = 2
     length = max(1, min(size // capacity, 512 // capacity)) * capacity
     return pl.pallas_call(
-        functools.partial(relay_kernel, cut, slabs, parts),
+        functools.partial(relay_kernel, cut, slabs),
         out_shape=[
             pltpu.VMEM((rows // width, 8, width), F32),
             jax.ShapeDtypeStruct((groups, 8, 128), jnp.int32),
@@ -289,7 +281,7 @@
         + [
             pltpu.VMEM((devices, 8, capacity), F32),
             pltpu.VMEM((capacity, sens.shape[1]), BF16),
-            pltpu.VMEM((devices // parts * 16, sens.shape[1]), BF16),
+            pltpu.VMEM((devices * 2 * SENT, sens.shape[1]), BF16),
             pltpu.SemaphoreType.DMA((6,)),
         ]
         + [pltpu.SemaphoreType.DMA((devices,))] * 2,
@@ -423,7 +415,7 @@
         blocks = joined([late.at[group * senders + i] for i in range(senders)], SENT, FIELDS)
         lines = [spots[q : q + 1] for q in range(group * len(blocks), (group + 1) * len(blocks))]
         for t, tile in enumerate(ordered(blocks, lines, per_group, width)):
-            marks[group * per_group + t] = tile
+            marks[group * per_group + t, : FIELDS - SENT] = tile
 
     stage[0] = jnp.zeros(stage.shape[1:], F32)
     slabs = lax.fori_loop(0, steps // 2, deposit, tuple(jnp.int32(-1) for _ in range(groups)), unroll=8)
@@ -540,10 +532,10 @@
         def line(field):
             return jnp.concatenate([marks[t, field : field + 1] for t in numbers], axis=1)
 
-        owner, slot = split(line(5).astype(jnp.int32), BOX_DEV)
+        owner, slot = split(line(1).astype(jnp.int32), BOX_DEV)
         rows = jnp.concatenate(
             [found[t // per_group * steps + slab_of[t // per_group, 1, t % per_group]][:parts] for t in numbers], axis=1
-        ) * line(4)
+        ) * line(0)
         at_owner = matches(devices, owner)
         pairs = [two_terms(rows[k : k + 1]) for k in range(parts)]
         values = [hi for hi, lo in pairs] + [lo for hi, lo in pairs]

time: 62 us -> 59.4 us (0.958)
  Pallas kernels: 59.4 us -> 56.8 us
    pallas_call x1, Pallas kernels: 22.3 us -> 20.1 us  [relay_rows(): pl.pallas_call(functools.partial(relay_kernel, cut, slabs), out_shape=[pl...]
where the time goes in v7:
time: 59.4 us; the launch traced here: 59.2 us
  Pallas kernels  56.8 us (96%)
  local copies, waits for them, and re-layouts  1.72 us (3%)
  between operations  0.65 us (1%)
    pallas_call x1, Pallas kernels, solve_rows(): pl.pallas_call(solve_kernel, out_shape=[pltpu.VMEM(anchor.shape, F32), pl...  36.7 us
    pallas_call x1, Pallas kernels, relay_rows(): pl.pallas_call(functools.partial(relay_kernel, cut, slabs), out_shape=[pl...  20.1 us
    unnamed x2, local copies, waits for them, and re-layouts  1.72 us

profile of v7, /device:TPU:0, one launch (start us, length us, event | category | flops | bytes accessed | tf_op | source)
XLA Modules:
  0.0 59.2 jit_solution(11577538442338741670)
XLA Ops:
  0.6 20.1 %relay_rows.1 = (f32[64,8,256]{2,1,0:T(8,128)S(1)}, s32[4,8,128]{2,1,0:T(8,128)}, s32[32,512]{1,0:T(8,128)S(1)}, f32[32,8,512]{2,1,0:T(8,128)S(1)}) custom-call(f32[3,8192]{1,0:T(4,128)} %refs_0_.1, f32[1,8192]{1,0:T(1,128)} %bitcast.5, s32[1,8192]{1,0:T(1,128)} %bitcast.6, s32[1,8192]{1,0:T(1,128)} %bitcast.7, s32[1,8192]{1,0:T(1,128)} %bitcast.8, ...), custom_call_target="tpu_custom_call" | custom-call | tf_op jit(solution)/shard_map/relay_rows/pallas_call | solution.py:270
  20.8 36.7 %solve_rows.1 = (f32[3,16,32,256]{3,2,1,0:T(8,128)S(1)}, f32[3,64]{1,0:T(4,128)S(1)}) custom-call(s32[4,8,128]{2,1,0:T(8,128)} %get-tuple-element.6.slab_of, f32[64,8,256]{2,1,0:T(8,128)S(1)} %get-tuple-element.7.tiles, s32[32,512]{1,0:T(8,128)S(1)} %get-tuple-element.8.spots, f32[32,8,512]{2,1,0:T(8,128)S(1)} %get-tuple-element.9.parcels, ...), custom_call_target="tpu_custom_call" | custom-call | tf_op jit(solution)/shard_map/solve_rows/pallas_call | solution.py:601
  57.5 1.1 %copy.13 = f32[3,16,32,256]{3,2,1,0:T(8,128)} copy(f32[3,16,32,256]{3,2,1,0:T(8,128)S(1)} %get-tuple-element.10) | data formatting | bytes 3145728
  58.6 0.6 copy.14

commit v8 on v7

--- a/solution.py
+++ b/solution.py
@@ -162,18 +162,20 @@
         rank = picked(chosen[q], before[q] + total[q][:, :1]).astype(jnp.int32)
         place[:, span] = wide_one_hot(capacity, rank)
 
-    def copy(step):
+    senders = count // groups
+
+    def copy(step, size):
         return pltpu.make_async_remote_copy(
-            src_ref=send.at[step, pl.ds(0, SENT)],
-            dst_ref=recv.at[step, pl.ds(0, SENT)],
-            send_sem=send_sem.at[step],
-            recv_sem=recv_sem.at[step],
+            src_ref=send.at[pl.ds(step, size), pl.ds(0, SENT)],
+            dst_ref=recv.at[pl.ds(step, size), pl.ds(0, SENT)],
+            send_sem=send_sem.at[0],
+            recv_sem=recv_sem.at[step // senders],
             device_id=peer(step),
             device_id_type=MESH,
         )
 
     def start(step, carry):
-        copy(step).start()
+        copy(step, 1).start()
         return carry
 
     def packed(rows, low):
@@ -190,20 +192,12 @@
     packed([lambda span: weight[:, span], lambda span: (owner[:, span] * BOX_DEV + slot[:, span]).astype(F32)], SENT)
     recv[0] = send[0]
 
-    def arrive(step, carry):
-        copy(step).wait_recv()
-        return carry
-
-    senders = count // groups
     for group in range(groups):
-        lax.fori_loop(max(1, group * senders), (group + 1) * senders, arrive, 0)
+        begin = max(1, group * senders)
+        copy(begin, (group + 1) * senders - begin).wait_recv()
         sort_group(cut, slabs, [recv.at[group * senders + i] for i in range(senders)], tiles, group * per_group, per_group, slab_of, spots, group)
 
-    def sent(step, carry):
-        copy(step).wait_send()
-        return carry
-
-    lax.fori_loop(1, count, sent, 0)
+    copy(1, count - 1).wait_send()
 
 
 def joined(arrived, low, high):
@@ -283,8 +277,9 @@
             pltpu.VMEM((capacity, sens.shape[1]), BF16),
             pltpu.VMEM((devices * 2 * SENT, sens.shape[1]), BF16),
             pltpu.SemaphoreType.DMA((6,)),
-        ]
-        + [pltpu.SemaphoreType.DMA((devices,))] * 2,
+            pltpu.SemaphoreType.DMA((1,)),
+            pltpu.SemaphoreType.DMA((groups,)),
+        ],
         compiler_params=pltpu.CompilerParams(collective_id=1, has_side_effects=True, vmem_limit_bytes=60 << 20),
         name="relay_rows",
     )(sens, weight, device, cell, owner, slot)
@@ -392,22 +387,18 @@
 
     late_rows = pl.ds(SENT, FIELDS - SENT)
 
-    def follow(step):
+    def follow(step, size):
         return pltpu.make_async_remote_copy(
-            src_ref=parcels.at[step, late_rows],
-            dst_ref=late.at[step, late_rows],
-            send_sem=late_send.at[step],
-            recv_sem=late_recv.at[step],
+            src_ref=parcels.at[pl.ds(step, size), late_rows],
+            dst_ref=late.at[pl.ds(step, size), late_rows],
+            send_sem=late_send.at[0],
+            recv_sem=late_recv.at[0],
             device_id=peer(step),
             device_id_type=MESH,
         )
 
     def send_late(step, carry):
-        follow(devices - step).start()
-        return carry
-
-    def take_late(step, carry):
-        follow(step).wait_recv()
+        follow(devices - step, 1).start()
         return carry
 
     def sort_late(group):
@@ -449,7 +440,7 @@
 
     lax.fori_loop(0, size_x, first, 0)
     begin(0)
-    lax.fori_loop(1, devices, take_late, 0)
+    follow(1, devices - 1).wait_recv()
 
     for index in range(exchanges):
         last = index + 1 == exchanges
@@ -545,43 +536,31 @@
         part = total[k * devices : (k + 1) * devices] + total[(parts + k) * devices : (parts + k + 1) * devices]
         flat[k] = jnp.concatenate([part, jnp.zeros_like(part)], axis=1)
 
-    def parcel(step):
+    def parcel(step, first, size):
         there = peer(step)
         return pltpu.make_async_remote_copy(
-            src_ref=flat.at[:, pl.ds(there[0] * count_y + there[1], 1)],
-            dst_ref=landed.at[:, pl.ds(step, 1)],
-            send_sem=box_send.at[step],
-            recv_sem=box_recv.at[step],
+            src_ref=flat.at[:, pl.ds(first, size)],
+            dst_ref=landed.at[:, pl.ds(step, size)],
+            send_sem=box_send.at[0],
+            recv_sem=box_recv.at[0],
             device_id=there,
             device_id_type=MESH,
         )
 
     def post(step, carry):
-        parcel(devices - step).start()
+        there = peer(devices - step)
+        parcel(devices - step, there[0] * count_y + there[1], 1).start()
         return carry
 
     lax.fori_loop(1, devices, post, 0)
     landed[:, 0:1] = flat[:, pl.ds(gx * count_y + gy, 1)]
 
-    def collect(step, carry):
-        parcel(step).wait_recv()
-        return carry
-
-    lax.fori_loop(1, devices, collect, 0)
+    parcel(1, 1, devices - 1).wait_recv()
     for k in range(parts):
         box[k : k + 1] = jnp.sum(landed[k], axis=0, keepdims=True)[:, :BOX_DEV]
 
-    def sent(step, carry):
-        parcel(step).wait_send()
-        return carry
-
-    lax.fori_loop(1, devices, sent, 0)
-
-    def left(step, carry):
-        follow(step).wait_send()
-        return carry
-
-    lax.fori_loop(1, devices, left, 0)
+    parcel(1, 1, devices - 1).wait_send()
+    follow(1, devices - 1).wait_send()
     for index in range(exchanges):
         for present, copy in transfers(index, True):
 
@@ -624,12 +603,35 @@
             pltpu.VMEM((parts, devices, 2 * BOX_DEV), F32),
             pltpu.SemaphoreType.DMA((3,)),
         ]
-        + [pltpu.SemaphoreType.DMA((devices,))] * 2
+        + [pltpu.SemaphoreType.DMA((1,))] * 2
         + [pltpu.SemaphoreType.DMA((exchanges, 2))] * 4
-        + [pltpu.SemaphoreType.DMA((devices,))] * 2,
+        + [pltpu.SemaphoreType.DMA((1,))] * 2,
         compiler_params=pltpu.CompilerParams(collective_id=0, has_side_effects=True, vmem_limit_bytes=56 << 20),
         name="solve_rows",
     )(slab_of, *kept_near, stiffness, anchor, coupling)
+
+
+def hand_kernel(adjoint, box, adjoint_out, box_out, sem):
+    copies = [
+        pltpu.make_async_copy(adjoint, adjoint_out, sem.at[0]),
+        pltpu.make_async_copy(box, box_out, sem.at[1]),
+    ]
+    for copy in copies:
+        copy.start()
+    for copy in copies:
+        copy.wait()
+
+
+def hand_over(adjoint, box):
+    values = [pltpu.with_memory_space_constraint(value, pltpu.VMEM) for value in (adjoint, box)]
+    return pl.pallas_call(
+        hand_kernel,
+        out_shape=[jax.ShapeDtypeStruct(value.shape, F32) for value in values],
+        in_specs=[pl.BlockSpec(memory_space=pltpu.VMEM)] * 2,
+        out_specs=[pl.BlockSpec(memory_space=pltpu.HBM)] * 2,
+        scratch_shapes=[pltpu.SemaphoreType.DMA((2,))],
+        name="hand_over",
+    )(*values)
 
 
 def body(
@@ -665,7 +667,7 @@
         row(box_owner),
         row(box_slot),
     )
-    adjoint, box_gradient = solve_rows(devices, tiles, slab_of, spots, parcels, stiffness, anchor, coupling)
+    adjoint, box_gradient = hand_over(*solve_rows(devices, tiles, slab_of, spots, parcels, stiffness, anchor, coupling))
     return (adjoint, box_gradient)
 
 

time: 59.4 us -> 56.7 us (0.955)
  local copies, waits for them, and re-layouts: 1.72 us -> 0 us
  Pallas kernels: 56.8 us -> 55.6 us
    unnamed x2 -> x0, local copies, waits for them, and re-layouts: 1.72 us -> none
    pallas_call x1, Pallas kernels: 36.7 us -> 35.3 us  [solve_rows(): pl.pallas_call(solve_kernel, out_shape=[pltpu.VMEM(anchor.shape, F32), pl...]
    pallas_call x0 -> x1, Pallas kernels: none -> 1.16 us  [hand_over(): pl.pallas_call(hand_kernel, out_shape=[jax.ShapeDtypeStruct(value.shape,...]
    pallas_call x1, Pallas kernels: 20.1 us -> 19.2 us  [relay_rows(): pl.pallas_call(functools.partial(relay_kernel, cut, slabs), out_shape=[pl...]
where the time goes in v8:
time: 56.7 us; the launch traced here: 56.4 us
  Pallas kernels  55.6 us (98%)
  between operations  0.81 us (1%)
    pallas_call x1, Pallas kernels, solve_rows(): pl.pallas_call(solve_kernel, out_shape=[pltpu.VMEM(anchor.shape, F32), pl...  35.3 us
    pallas_call x1, Pallas kernels, relay_rows(): pl.pallas_call(functools.partial(relay_kernel, cut, slabs), out_shape=[pl...  19.2 us
    pallas_call x1, Pallas kernels, hand_over(): pl.pallas_call(hand_kernel, out_shape=[jax.ShapeDtypeStruct(value.shape,...  1.16 us

profile of v8, /device:TPU:0, one launch (start us, length us, event | category | flops | bytes accessed | tf_op | source)
XLA Modules:
  0.0 56.4 jit_solution(9853368648549183742)
XLA Ops:
  0.6 19.2 %relay_rows.1 = (f32[64,8,256]{2,1,0:T(8,128)S(1)}, s32[4,8,128]{2,1,0:T(8,128)}, s32[32,512]{1,0:T(8,128)S(1)}, f32[32,8,512]{2,1,0:T(8,128)S(1)}) custom-call(f32[3,8192]{1,0:T(4,128)} %refs_0_.1, f32[1,8192]{1,0:T(1,128)} %bitcast.5, s32[1,8192]{1,0:T(1,128)} %bitcast.6, s32[1,8192]{1,0:T(1,128)} %bitcast.7, s32[1,8192]{1,0:T(1,128)} %bitcast.8, ...), custom_call_target="tpu_custom_call" | custom-call | tf_op jit(solution)/shard_map/relay_rows/pallas_call | solution.py:264
  19.8 35.3 %solve_rows.1 = (f32[3,16,32,256]{3,2,1,0:T(8,128)S(1)}, f32[3,64]{1,0:T(4,128)S(1)}) custom-call(s32[4,8,128]{2,1,0:T(8,128)} %get-tuple-element.8.slab_of, f32[64,8,256]{2,1,0:T(8,128)S(1)} %get-tuple-element.9.tiles, s32[32,512]{1,0:T(8,128)S(1)} %get-tuple-element.10.spots, f32[32,8,512]{2,1,0:T(8,128)S(1)} %get-tuple-element.11.parcels, ...), custom_call_target="tpu_custom_call" | custom-call | tf_op jit(solution)/shard_map/solve_rows/pallas_call | solution.py:580
  55.1 1.2 %hand_over.1 = (f32[3,16,32,256]{3,2,1,0:T(8,128)}, f32[3,64]{1,0:T(4,128)}) custom-call(f32[3,16,32,256]{3,2,1,0:T(8,128)S(1)} %get-tuple-element.12.adjoint, f32[3,64]{1,0:T(4,128)S(1)} %get-tuple-element.13.box), custom_call_target="tpu_custom_call" | custom-call | tf_op jit(solution)/shard_map/hand_over/pallas_call | solution.py:627

commit v9 on v8

--- a/solution.py
+++ b/solution.py
@@ -84,8 +84,9 @@
     return total
 
 
-def peer_of(gx, gy, size_x, size_y):
-    return lambda step: (folded(gx, step // size_y, size_x), (gy + step % size_y) % size_y)
+def peers_of(gx, gy, size_x, size_y):
+    along = [(gy + step) % size_y for step in range(size_y)]
+    return [(across, there) for across in [folded(gx, step, size_x) for step in range(size_x)] for there in along]
 
 
 def running(numbers):
@@ -126,7 +127,7 @@
     per_group = tiles.shape[0] // groups
     gx, gy = lax.axis_index("gx"), lax.axis_index("gy")
     size_x, size_y = lax.axis_size("gx"), lax.axis_size("gy")
-    peer = peer_of(gx, gy, size_x, size_y)
+    peers = peers_of(gx, gy, size_x, size_y)
     barrier = pltpu.get_barrier_semaphore()
     fetches = [
         pltpu.make_async_copy(source, target, fetch.at[i])
@@ -135,11 +136,8 @@
     for copy in fetches:
         copy.start()
 
-    def greet(step, carry):
-        pl.semaphore_signal(barrier, inc=1, device_id=peer(step), device_id_type=MESH)
-        return carry
-
-    lax.fori_loop(1, count, greet, 0)
+    for peer in peers[1:]:
+        pl.semaphore_signal(barrier, inc=1, device_id=peer, device_id_type=MESH)
 
     length = min(512, rows)
     chunks = rows // length
@@ -170,13 +168,9 @@
             dst_ref=recv.at[pl.ds(step, size), pl.ds(0, SENT)],
             send_sem=send_sem.at[0],
             recv_sem=recv_sem.at[step // senders],
-            device_id=peer(step),
+            device_id=peers[step],
             device_id_type=MESH,
         )
-
-    def start(step, carry):
-        copy(step, 1).start()
-        return carry
 
     def packed(rows, low):
         size = 2 * len(rows)
@@ -188,7 +182,8 @@
 
     packed([lambda span, k=k: sens[k : k + 1, span] for k in range(3)] + [lambda span: cell[:, span].astype(F32)], 0)
     pl.semaphore_wait(barrier, count - 1)
-    lax.fori_loop(1, count, start, 0)
+    for step in range(1, count):
+        copy(step, 1).start()
     packed([lambda span: weight[:, span], lambda span: (owner[:, span] * BOX_DEV + slot[:, span]).astype(F32)], SENT)
     recv[0] = send[0]
 
@@ -300,17 +295,14 @@
     gx, gy = lax.axis_index("gx"), lax.axis_index("gy")
     count_x, count_y = lax.axis_size("gx"), lax.axis_size("gy")
     devices = count_x * count_y
-    peer = peer_of(gx, gy, count_x, count_y)
+    peers = peers_of(gx, gy, count_x, count_y)
     sides = (("gx", gx, -1, gx > 0), ("gx", gx, 1, gx < count_x - 1), ("gy", gy, -1, gy > 0), ("gy", gy, 1, gy < count_y - 1))
     y_at = lax.broadcasted_iota(jnp.int32, (size_y, size_z), 0)
     z_at = lax.broadcasted_iota(jnp.int32, (size_y, size_z), 1)
     barrier = pltpu.get_barrier_semaphore()
 
-    def greet(step, carry):
-        pl.semaphore_signal(barrier, inc=1, device_id=peer(step), device_id_type=MESH)
-        return carry
-
-    lax.fori_loop(1, devices, greet, 0)
+    for peer in peers[1:]:
+        pl.semaphore_signal(barrier, inc=1, device_id=peer, device_id_type=MESH)
     fetches = [
         pltpu.make_async_copy(source, target, fetch.at[i])
         for i, (source, target) in enumerate(((stiff_in, stiff), (anchor_in, anchor), (coupling_in, coupling)))
@@ -393,13 +385,9 @@
             dst_ref=late.at[pl.ds(step, size), late_rows],
             send_sem=late_send.at[0],
             recv_sem=late_recv.at[0],
-            device_id=peer(step),
+            device_id=peers[step],
             device_id_type=MESH,
         )
-
-    def send_late(step, carry):
-        follow(devices - step, 1).start()
-        return carry
 
     def sort_late(group):
         senders = devices // groups
@@ -411,7 +399,8 @@
     stage[0] = jnp.zeros(stage.shape[1:], F32)
     slabs = lax.fori_loop(0, steps // 2, deposit, tuple(jnp.int32(-1) for _ in range(groups)), unroll=8)
     pl.semaphore_wait(barrier, devices - 1)
-    lax.fori_loop(1, devices, send_late, 0)
+    for step in reversed(range(1, devices)):
+        follow(step, 1).start()
     late[0] = parcels[0]
     lax.fori_loop(steps // 2, steps, deposit, slabs, unroll=8)
     for copy in fetches:
@@ -537,22 +526,18 @@
         flat[k] = jnp.concatenate([part, jnp.zeros_like(part)], axis=1)
 
     def parcel(step, first, size):
-        there = peer(step)
         return pltpu.make_async_remote_copy(
             src_ref=flat.at[:, pl.ds(first, size)],
             dst_ref=landed.at[:, pl.ds(step, size)],
             send_sem=box_send.at[0],
             recv_sem=box_recv.at[0],
-            device_id=there,
+            device_id=peers[step],
             device_id_type=MESH,
         )
 
-    def post(step, carry):
-        there = peer(devices - step)
-        parcel(devices - step, there[0] * count_y + there[1], 1).start()
-        return carry
-
-    lax.fori_loop(1, devices, post, 0)
+    for step in reversed(range(1, devices)):
+        there = peers[step]
+        parcel(step, there[0] * count_y + there[1], 1).start()
     landed[:, 0:1] = flat[:, pl.ds(gx * count_y + gy, 1)]
 
     parcel(1, 1, devices - 1).wait_recv()

time: 56.7 us -> 54.5 us (0.961)
  Pallas kernels: 55.6 us -> 53.4 us
    pallas_call x1, Pallas kernels: 35.3 us -> 34.1 us  [solve_rows(): pl.pallas_call(solve_kernel, out_shape=[pltpu.VMEM(anchor.shape, F32), pl...]
    pallas_call x1, Pallas kernels: 19.2 us -> 18.2 us  [relay_rows(): pl.pallas_call(functools.partial(relay_kernel, cut, slabs), out_shape=[pl...]
where the time goes in v9:
time: 54.5 us; the launch traced here: 54.2 us
  Pallas kernels  53.4 us (98%)
  between operations  0.81 us (1%)
    pallas_call x1, Pallas kernels, solve_rows(): pl.pallas_call(solve_kernel, out_shape=[pltpu.VMEM(anchor.shape, F32), pl...  34.1 us
    pallas_call x1, Pallas kernels, relay_rows(): pl.pallas_call(functools.partial(relay_kernel, cut, slabs), out_shape=[pl...  18.2 us
    pallas_call x1, Pallas kernels, hand_over(): pl.pallas_call(hand_kernel, out_shape=[jax.ShapeDtypeStruct(value.shape,...  1.16 us

profile of v9, /device:TPU:0, one launch (start us, length us, event | category | flops | bytes accessed | tf_op | source)
XLA Modules:
  0.0 54.2 jit_solution(15158250632077237501)
XLA Ops:
  0.6 18.2 %relay_rows.1 = (f32[64,8,256]{2,1,0:T(8,128)S(1)}, s32[4,8,128]{2,1,0:T(8,128)}, s32[32,512]{1,0:T(8,128)S(1)}, f32[32,8,512]{2,1,0:T(8,128)S(1)}) custom-call(f32[3,8192]{1,0:T(4,128)} %refs_0_.1, f32[1,8192]{1,0:T(1,128)} %bitcast.5, s32[1,8192]{1,0:T(1,128)} %bitcast.6, s32[1,8192]{1,0:T(1,128)} %bitcast.7, s32[1,8192]{1,0:T(1,128)} %bitcast.8, ...), custom_call_target="tpu_custom_call" | custom-call | tf_op jit(solution)/shard_map/relay_rows/pallas_call | solution.py:259
  18.8 34.1 %solve_rows.1 = (f32[3,16,32,256]{3,2,1,0:T(8,128)S(1)}, f32[3,64]{1,0:T(4,128)S(1)}) custom-call(s32[4,8,128]{2,1,0:T(8,128)} %get-tuple-element.8.slab_of, f32[64,8,256]{2,1,0:T(8,128)S(1)} %get-tuple-element.9.tiles, s32[32,512]{1,0:T(8,128)S(1)} %get-tuple-element.10.spots, f32[32,8,512]{2,1,0:T(8,128)S(1)} %get-tuple-element.11.parcels, ...), custom_call_target="tpu_custom_call" | custom-call | tf_op jit(solution)/shard_map/solve_rows/pallas_call | solution.py:565
  52.9 1.2 %hand_over.1 = (f32[3,16,32,256]{3,2,1,0:T(8,128)}, f32[3,64]{1,0:T(4,128)}) custom-call(f32[3,16,32,256]{3,2,1,0:T(8,128)S(1)} %get-tuple-element.12.adjoint, f32[3,64]{1,0:T(4,128)S(1)} %get-tuple-element.13.box), custom_call_target="tpu_custom_call" | custom-call | tf_op jit(solution)/shard_map/hand_over/pallas_call | solution.py:612

commit v10 on v9

--- a/solution.py
+++ b/solution.py
@@ -397,12 +397,12 @@
             marks[group * per_group + t, : FIELDS - SENT] = tile
 
     stage[0] = jnp.zeros(stage.shape[1:], F32)
-    slabs = lax.fori_loop(0, steps // 2, deposit, tuple(jnp.int32(-1) for _ in range(groups)), unroll=8)
+    slabs = lax.fori_loop(0, steps // 2, deposit, tuple(jnp.int32(-1) for _ in range(groups)), unroll=16)
     pl.semaphore_wait(barrier, devices - 1)
     for step in reversed(range(1, devices)):
         follow(step, 1).start()
     late[0] = parcels[0]
-    lax.fori_loop(steps // 2, steps, deposit, slabs, unroll=8)
+    lax.fori_loop(steps // 2, steps, deposit, slabs, unroll=16)
     for copy in fetches:
         copy.wait()
 

time: 54.5 us -> 54 us (level)
  no operation moved by 1% of the time
where the time goes in v10:
time: 54 us; the launch traced here: 53.7 us
  Pallas kernels  52.9 us (98%)
  between operations  0.81 us (2%)
    pallas_call x1, Pallas kernels, solve_rows(): pl.pallas_call(solve_kernel, out_shape=[pltpu.VMEM(anchor.shape, F32), pl...  33.5 us
    pallas_call x1, Pallas kernels, relay_rows(): pl.pallas_call(functools.partial(relay_kernel, cut, slabs), out_shape=[pl...  18.2 us
    pallas_call x1, Pallas kernels, hand_over(): pl.pallas_call(hand_kernel, out_shape=[jax.ShapeDtypeStruct(value.shape,...  1.16 us

profile of v10, /device:TPU:0, one launch (start us, length us, event | category | flops | bytes accessed | tf_op | source)
XLA Modules:
  0.0 53.7 jit_solution(3953939164096243496)
XLA Ops:
  0.6 18.2 %relay_rows.1 = (f32[64,8,256]{2,1,0:T(8,128)S(1)}, s32[4,8,128]{2,1,0:T(8,128)}, s32[32,512]{1,0:T(8,128)S(1)}, f32[32,8,512]{2,1,0:T(8,128)S(1)}) custom-call(f32[3,8192]{1,0:T(4,128)} %refs_0_.1, f32[1,8192]{1,0:T(1,128)} %bitcast.5, s32[1,8192]{1,0:T(1,128)} %bitcast.6, s32[1,8192]{1,0:T(1,128)} %bitcast.7, s32[1,8192]{1,0:T(1,128)} %bitcast.8, ...), custom_call_target="tpu_custom_call" | custom-call | tf_op jit(solution)/shard_map/relay_rows/pallas_call | solution.py:259
  18.8 33.5 %solve_rows.1 = (f32[3,16,32,256]{3,2,1,0:T(8,128)S(1)}, f32[3,64]{1,0:T(4,128)S(1)}) custom-call(s32[4,8,128]{2,1,0:T(8,128)} %get-tuple-element.8.slab_of, f32[64,8,256]{2,1,0:T(8,128)S(1)} %get-tuple-element.9.tiles, s32[32,512]{1,0:T(8,128)S(1)} %get-tuple-element.10.spots, f32[32,8,512]{2,1,0:T(8,128)S(1)} %get-tuple-element.11.parcels, ...), custom_call_target="tpu_custom_call" | custom-call | tf_op jit(solution)/shard_map/solve_rows/pallas_call | solution.py:565
  52.4 1.2 %hand_over.1 = (f32[3,16,32,256]{3,2,1,0:T(8,128)}, f32[3,64]{1,0:T(4,128)}) custom-call(f32[3,16,32,256]{3,2,1,0:T(8,128)S(1)} %get-tuple-element.12.adjoint, f32[3,64]{1,0:T(4,128)S(1)} %get-tuple-element.13.box), custom_call_target="tpu_custom_call" | custom-call | tf_op jit(solution)/shard_map/hand_over/pallas_call | solution.py:612
